TPU v7x, 32 devices: a whole 2x2x4 slice. The times are simulated.
32 devices in a mesh: group: 4 (over z_hi, core), blk: 4 (over y, x), head: 2 (over z_lo).
Axes of the slice: x: 2, y: 2, z: 4 (z_hi: 2, z_lo: 2; z = z_hi * 2 + z_lo), core: 2. Of those that a mesh axis runs over, the one named last changes fastest.
Arguments:
- tokens: bfloat16 [8, 1024, 1024], P('group', ('blk', 'head')), may hold values from -6 to 6
- segments: int32 [8, 1024], P('group'), may hold values from 0 to 7, never falling along the last dimension, each value on 1 to 512 neighbouring positions
- routes: int32 [8, 1024, 8], P('group', ('blk', 'head')), may hold values from 0 to 31, all different within a row; in each aligned block of 128 rows (0 to 127, 128 to 255, ..., all dimensions but the last counted through in order) at most 36 rows name the same one
- cotangent: bfloat16 [8, 1024, 1024], P('group', ('blk', 'head')), may hold values from -6 to 6
- attn_gain: bfloat16 [1024], P(('blk', 'head')), may hold values from 0.5 to 1.5
- moe_gain: bfloat16 [1024], P(('blk', 'head')), may hold values from 0.5 to 1.5
- query_weight: bfloat16 [1024, 1024], P(('blk', 'head')), may hold values from -0.1875 to 0.1875
- key_projection_matrix: bfloat16 [1024, 512], P(('blk', 'head')), may hold values from -0.1875 to 0.1875
- value_projection_matrix: bfloat16 [1024, 512], P(('blk', 'head')), may hold values from -0.1875 to 0.1875
- out_weight: bfloat16 [1024, 1024], P(('blk', 'head')), may hold values from -1.5 to 1.5
- router_weight: bfloat16 [1024, 32], P(('blk', 'head')), may hold values from -0.375 to 0.375
- gate_weight: bfloat16 [32, 1024, 512], P(('blk', 'head')), may hold values from -0.1875 to 0.1875
- up_weight: bfloat16 [32, 1024, 512], P(('blk', 'head')), may hold values from -0.1875 to 0.1875
- down_weight: bfloat16 [32, 512, 1024], P(('blk', 'head')), may hold values from -0.75 to 0.75
Outputs:
- mixed: bfloat16 [8, 1024, 1024], P('group', ('blk', 'head'))
- token_grad: float32 [8, 1024, 1024], P('group', ('blk', 'head'))
- attn_gain_grad: float32 [1024], P(('blk', 'head'))
- moe_gain_grad: float32 [1024], P(('blk', 'head'))
- query_weight_grad: float32 [1024, 1024], P(('blk', 'head'))
- key_weight_grad: float32 [1024, 512], P(('blk', 'head'))
- value_weight_grad: float32 [1024, 512], P(('blk', 'head'))
- out_weight_grad: float32 [1024, 1024], P(('blk', 'head'))
- router_weight_grad: float32 [1024, 32], P(('blk', 'head'))
- gate_weight_grad: float32 [32, 1024, 512], P(('blk', 'head'))
- up_weight_grad: float32 [32, 1024, 512], P(('blk', 'head'))
- down_weight_grad: float32 [32, 512, 1024], P(('blk', 'head'))
Inputs may be any that keep to these rules, and one draw needn't show every extreme that they name: `routes`: each row names 8 distinct experts; in each aligned block of 128 positions of a sequence no expert is named by more than 36 rows, a bound that some block reaches. `segments`: within each sequence the numbers never fall; each document has at most 512 positions, and one has exactly 512.
All inputs are finite; a program needn't handle non-finite values.
Results may differ from a plain program's by a relative error of at most 0.03.
Values may be sent and summed in bfloat16 or wider, within the bound.
A program may use at most 192 MiB of HBM per device.

v0:
```python
import functools

import jax
import jax.numpy as jnp
import numpy as np
from jax import lax
from jax.experimental import pallas as pl
from jax.experimental.pallas import tpu as pltpu
from jax.sharding import PartitionSpec as P

QUERY_HEADS = 16
KEY_VALUE_HEADS = 8
HEAD_SIZE = 64
TOP = 8
CAPH = 36


epsilon = 1e-05
rope_base = 10000.0
masked_out = -1e30
key_block = 512


def rms_norm(values, gain_vec):
    return values * lax.rsqrt(jnp.mean(values * values, -1, keepdims=True) + epsilon) * gain_vec


def rotary_embedding(field_vals, places, turn_sign):
    half_dim = field_vals.shape[-1] // 2
    frequency = rope_base ** (-jnp.arange(half_dim, dtype=jnp.float32) * 2.0 / field_vals.shape[-1])
    angles = places.astype(jnp.float32)[:, None] * frequency[None, :]
    cosine = jnp.cos(angles)[:, None, :]
    sine_vals = turn_sign * jnp.sin(angles)[:, None, :]
    first_half = field_vals[..., :half_dim]
    second = field_vals[..., half_dim:]
    return jnp.concatenate(
        [first_half * cosine - second * sine_vals, second * cosine + first_half * sine_vals], -1
    )


def add_rows(running, addend, row_start):
    current = lax.dynamic_slice_in_dim(running, row_start, addend.shape[1], 1)
    return lax.dynamic_update_slice_in_dim(running, current + addend, row_start, 1)


def on_device(
    tokens,
    segments,
    routes,
    cotangent,
    attn_gain,
    moe_gain,
    query_weight,
    key_projection_matrix,
    value_projection_matrix,
    out_weight,
    router_weight,
    gate_weight,
    up_weight,
    down_weight,
):
    head_groups, number_of_rows, width_dim = tokens.shape
    query_per_key_head = QUERY_HEADS // KEY_VALUE_HEADS
    shared_head_count = lax.axis_size("head")
    query_rows = number_of_rows * shared_head_count
    grouped_keys = KEY_VALUE_HEADS // shared_head_count
    scale_val = HEAD_SIZE ** (-0.5)
    number_of_tokens = head_groups * number_of_rows
    seq_length = lax.axis_size("blk") * query_rows
    cycle_index = lax.axis_index("blk")
    local_placement = (
        cycle_index * shared_head_count + lax.axis_index("head")
    ) * number_of_rows + jnp.arange(number_of_rows, dtype=jnp.int32)
    own_start = cycle_index * query_rows
    query_place = own_start + jnp.arange(query_rows, dtype=jnp.int32)
    query_doc = lax.dynamic_slice_in_dim(segments, own_start, query_rows, 1)
    query_full, key_full, value_full, out_full, router_full, gain_attn, gain_moe = (
        lax.all_gather(query_weight, ("blk", "head"), axis=0, tiled=True),
        lax.all_gather(key_projection_matrix, ("blk", "head"), axis=0, tiled=True),
        lax.all_gather(value_projection_matrix, ("blk", "head"), axis=0, tiled=True),
        lax.all_gather(out_weight, ("blk", "head"), axis=0, tiled=True),
        lax.all_gather(router_weight, ("blk", "head"), axis=0, tiled=True),
        lax.all_gather(attn_gain, ("blk", "head"), axis=0, tiled=True),
        lax.all_gather(moe_gain, ("blk", "head"), axis=0, tiled=True),
    )
    flat_rows = tokens.reshape(number_of_tokens, width_dim).astype(jnp.float32)
    attn_normed, attn_pull = jax.vjp(rms_norm, flat_rows, gain_attn.astype(jnp.float32))
    attn_in = attn_normed.astype(jnp.bfloat16)
    query_pre = jnp.dot(attn_in, query_full, preferred_element_type=jnp.float32)
    key_before_rotary = jnp.dot(attn_in, key_full, preferred_element_type=jnp.float32)
    value_low = (
        jnp.dot(attn_in, value_full, preferred_element_type=jnp.float32)
        .astype(jnp.bfloat16)
        .reshape(head_groups, number_of_rows, KEY_VALUE_HEADS * HEAD_SIZE)
    )
    query_low = (
        rotary_embedding(
            query_pre.reshape(head_groups, number_of_rows, QUERY_HEADS, HEAD_SIZE),
            local_placement,
            1.0,
        )
        .astype(jnp.bfloat16)
        .reshape(head_groups, number_of_rows, QUERY_HEADS * HEAD_SIZE)
    )
    key_low = (
        rotary_embedding(
            key_before_rotary.reshape(head_groups, number_of_rows, KEY_VALUE_HEADS, HEAD_SIZE),
            local_placement,
            1.0,
        )
        .astype(jnp.bfloat16)
        .reshape(head_groups, number_of_rows, KEY_VALUE_HEADS * HEAD_SIZE)
    )
    query_split, key_split, value_split = (
        lax.all_to_all(query_low, "head", split_axis=2, concat_axis=1, tiled=True),
        lax.all_to_all(key_low, "head", split_axis=2, concat_axis=1, tiled=True),
        lax.all_to_all(value_low, "head", split_axis=2, concat_axis=1, tiled=True),
    )
    query_vectors = query_split.reshape(
        head_groups, query_rows, grouped_keys, query_per_key_head, HEAD_SIZE
    )

    def key_view(source, offset, sub_rows):
        return lax.dynamic_slice_in_dim(source, offset, sub_rows, 1).reshape(
            head_groups, sub_rows, grouped_keys, HEAD_SIZE
        )

    def scored_at(query_part, key_row_block, q_place, q_doc, key_start, sub_rows):
        raw_scores = (
            jnp.einsum(
                "bqgrd,bkgd->bqgrk", query_part, key_row_block, preferred_element_type=jnp.float32
            )
            * scale_val
        )
        key_place = key_start + jnp.arange(sub_rows, dtype=jnp.int32)
        key_doc = lax.dynamic_slice_in_dim(segments, key_start, sub_rows, 1)
        allowed = (q_place[None, :, None] >= key_place[None, None, :]) & (
            q_doc[:, :, None] == key_doc[:, None, :]
        )
        return (raw_scores, allowed[:, :, None, None, :])

    def scored(key_row_block, key_start, sub_rows):
        return scored_at(query_vectors, key_row_block, query_place, query_doc, key_start, sub_rows)

    stats_shape = (head_groups, query_rows, grouped_keys, query_per_key_head)
    init_state = (
        jnp.full(stats_shape, masked_out, jnp.float32),
        jnp.zeros(stats_shape, jnp.float32),
        jnp.zeros(stats_shape + (HEAD_SIZE,), jnp.float32),
    )
    key_all, value_all = (
        lax.all_gather(key_split, "blk", axis=1, tiled=True),
        lax.all_gather(value_split, "blk", axis=1, tiled=True),
    )
    fold_state = init_state
    total_rows = key_all.shape[1]
    sub_rows = key_block

    def forward_one_block(block_state, block_index):
        offset = block_index * sub_rows
        key_row_block = key_view(key_all, offset, sub_rows)
        value_row_block = key_view(value_all, offset, sub_rows)
        raw_scores, allowed = scored(key_row_block, 0 + offset, sub_rows)
        running_max, running_sum, running_acc = block_state
        masked = jnp.where(allowed, raw_scores, masked_out)
        new_max = jnp.maximum(running_max, jnp.max(masked, -1))
        shrink = jnp.exp(running_max - new_max)
        weights_soft = jnp.where(allowed, jnp.exp(masked - new_max[..., None]), 0.0)
        new_sum = running_sum * shrink + jnp.sum(weights_soft, -1)
        new_acc = running_acc * shrink[..., None] + jnp.einsum(
            "bqgrk,bkgd->bqgrd",
            weights_soft.astype(jnp.bfloat16),
            value_row_block,
            preferred_element_type=jnp.float32,
        )
        return ((new_max, new_sum, new_acc), None)

    fold_state, unused = lax.scan(
        forward_one_block, fold_state, jnp.arange(total_rows // sub_rows, dtype=jnp.int32)
    )
    running_max, running_sum, running_acc = fold_state
    mix_heads = running_acc / running_sum[..., None]
    log_total = running_max + jnp.log(running_sum)
    mix_low = mix_heads.astype(jnp.bfloat16).reshape(
        head_groups, query_rows, grouped_keys * query_per_key_head * HEAD_SIZE
    )
    mix_tokens = lax.all_to_all(mix_low, "head", split_axis=1, concat_axis=2, tiled=True)
    attn_mix = mix_tokens.reshape(number_of_tokens, QUERY_HEADS * HEAD_SIZE)
    residual = flat_rows + jnp.dot(attn_mix, out_full, preferred_element_type=jnp.float32)
    moe_normed, moe_pull = jax.vjp(rms_norm, residual, gain_moe.astype(jnp.float32))
    moe_in = moe_normed.astype(jnp.bfloat16)
    logits = jnp.dot(moe_in, router_full, preferred_element_type=jnp.float32)
    route_flat = routes.reshape(number_of_tokens, TOP)
    experts_all = router_full.shape[1]
    choose = route_flat[:, :, None] == jnp.arange(experts_all, dtype=jnp.int32)[None, None, :]
    choose_float = choose.astype(jnp.float32)
    picked_logits = jnp.einsum("nke,ne->nk", choose_float, logits)
    route_weights = jax.nn.softmax(picked_logits, axis=-1)
    choose_whole = choose.astype(jnp.int32).reshape(head_groups, number_of_rows * TOP, experts_all)
    slot_rank = jnp.sum(jnp.cumsum(choose_whole, 1) * choose_whole, -1) - 1
    slot_index = (slot_rank + jnp.arange(head_groups, dtype=jnp.int32)[:, None] * CAPH).reshape(-1)
    targets = route_flat.reshape(-1)
    lane_count = head_groups * CAPH
    outgoing = (
        jnp.zeros((experts_all, lane_count, width_dim), jnp.bfloat16)
        .at[targets, slot_index]
        .set(jnp.repeat(moe_in, TOP, axis=0))
    )
    arrived = lax.all_to_all(outgoing, ("blk", "head"), split_axis=0, concat_axis=1, tiled=True)
    gate_val = jnp.einsum("end,edf->enf", arrived, gate_weight, preferred_element_type=jnp.float32)
    up_val = jnp.einsum("end,edf->enf", arrived, up_weight, preferred_element_type=jnp.float32)
    hidden_low = (jax.nn.silu(gate_val) * up_val).astype(jnp.bfloat16)
    expert_out = jnp.einsum(
        "enf,efd->end", hidden_low, down_weight, preferred_element_type=jnp.float32
    ).astype(jnp.bfloat16)
    returned = lax.all_to_all(expert_out, ("blk", "head"), split_axis=1, concat_axis=0, tiled=True)
    picked_rows = returned[targets, slot_index].reshape(number_of_tokens, TOP, width_dim)
    moe_out = jnp.einsum(
        "nk,nkd->nd", route_weights, picked_rows, preferred_element_type=jnp.float32
    )
    mixed = (
        (residual + moe_out).astype(jnp.bfloat16).reshape(head_groups, number_of_rows, width_dim)
    )
    grad_full = cotangent.reshape(number_of_tokens, width_dim).astype(jnp.float32)
    weight_grad = jnp.einsum(
        "nkd,nd->nk", picked_rows, grad_full, preferred_element_type=jnp.float32
    )
    pair_grad = (
        (route_weights[:, :, None] * grad_full[:, None, :])
        .astype(jnp.bfloat16)
        .reshape(number_of_tokens * TOP, width_dim)
    )
    grad_outgoing = jnp.zeros_like(outgoing).at[targets, slot_index].set(pair_grad)
    grad_arrived = lax.all_to_all(
        grad_outgoing, ("blk", "head"), split_axis=0, concat_axis=1, tiled=True
    )
    grad_hidden = jnp.einsum(
        "end,efd->enf", grad_arrived, down_weight, preferred_element_type=jnp.float32
    )
    sigmoid_val = jax.nn.sigmoid(gate_val)
    grad_gate = (
        grad_hidden * up_val * sigmoid_val * (1.0 + gate_val * (1.0 - sigmoid_val))
    ).astype(jnp.bfloat16)
    grad_up = (grad_hidden * gate_val * sigmoid_val).astype(jnp.bfloat16)
    down_weight_grad = jnp.einsum(
        "enf,end->efd", hidden_low, grad_arrived, preferred_element_type=jnp.float32
    )
    gate_weight_grad = jnp.einsum(
        "end,enf->edf", arrived, grad_gate, preferred_element_type=jnp.float32
    )
    up_weight_grad = jnp.einsum(
        "end,enf->edf", arrived, grad_up, preferred_element_type=jnp.float32
    )
    pair_back = (
        jnp.einsum("enf,edf->end", grad_gate, gate_weight, preferred_element_type=jnp.float32)
        + jnp.einsum("enf,edf->end", grad_up, up_weight, preferred_element_type=jnp.float32)
    ).astype(jnp.bfloat16)
    grad_returned = lax.all_to_all(
        pair_back, ("blk", "head"), split_axis=1, concat_axis=0, tiled=True
    )
    moe_in_grad = jnp.sum(
        grad_returned[targets, slot_index].reshape(number_of_tokens, TOP, width_dim),
        axis=1,
        dtype=jnp.float32,
    )
    mean_term = jnp.sum(route_weights * weight_grad, -1, keepdims=True)
    logit_grad = jnp.einsum("nk,nke->ne", route_weights * (weight_grad - mean_term), choose_float)
    router_grad = jnp.dot(moe_in.T, logit_grad, preferred_element_type=jnp.float32)
    moe_in_grad = moe_in_grad + jnp.dot(
        logit_grad, router_full.T, preferred_element_type=jnp.float32
    )
    residual_part, moe_gain_grad = moe_pull(moe_in_grad)
    residual_grad = grad_full + residual_part
    out_grad_low = residual_grad.astype(jnp.bfloat16)
    out_weight_grad = jnp.dot(attn_mix.T, out_grad_low, preferred_element_type=jnp.float32)
    mix_grad = (
        jnp.dot(out_grad_low, out_full.T, preferred_element_type=jnp.float32)
        .astype(jnp.bfloat16)
        .reshape(head_groups, number_of_rows, QUERY_HEADS * HEAD_SIZE)
    )
    mix_grad_heads = lax.all_to_all(
        mix_grad, "head", split_axis=2, concat_axis=1, tiled=True
    ).reshape(head_groups, query_rows, grouped_keys, query_per_key_head, HEAD_SIZE)
    delta_term = jnp.sum(mix_grad_heads.astype(jnp.float32) * mix_heads, -1)
    query_zero = jnp.zeros(stats_shape + (HEAD_SIZE,), jnp.float32)
    back_init = (
        query_zero,
        jnp.zeros((head_groups, seq_length, grouped_keys, HEAD_SIZE), jnp.float32),
        jnp.zeros((head_groups, seq_length, grouped_keys, HEAD_SIZE), jnp.float32),
    )
    fold_state = back_init
    total_rows = key_all.shape[1]

    def backward_one_block(block_state, block_index):
        offset = block_index * key_block
        key_start = 0 + offset
        key_row_block = key_view(key_all, offset, key_block)
        value_row_block = key_view(value_all, offset, key_block)
        raw_scores, allowed = scored(key_row_block, key_start, key_block)
        masked = jnp.where(allowed, raw_scores, masked_out)
        probability = jnp.where(allowed, jnp.exp(masked - log_total[..., None]), 0.0)
        prob_grad = jnp.einsum(
            "bqgrd,bkgd->bqgrk", mix_grad_heads, value_row_block, preferred_element_type=jnp.float32
        )
        score_grad = (probability * (prob_grad - delta_term[..., None]) * scale_val).astype(
            jnp.bfloat16
        )
        grad_query = block_state[0] + jnp.einsum(
            "bqgrk,bkgd->bqgrd", score_grad, key_row_block, preferred_element_type=jnp.float32
        )
        value_part_grad = jnp.einsum(
            "bqgrk,bqgrd->bkgd",
            probability.astype(jnp.bfloat16),
            mix_grad_heads,
            preferred_element_type=jnp.float32,
        )
        key_part_grad = jnp.einsum(
            "bqgrk,bqgrd->bkgd", score_grad, query_vectors, preferred_element_type=jnp.float32
        )
        grad_keys = add_rows(block_state[1], key_part_grad, key_start)
        grad_values = add_rows(block_state[2], value_part_grad, key_start)
        return ((grad_query, grad_keys, grad_values), None)

    fold_state, unused = lax.scan(
        backward_one_block, fold_state, jnp.arange(total_rows // key_block, dtype=jnp.int32)
    )
    grad_query, grad_keys, grad_values = fold_state
    key_own, value_own = (
        lax.psum_scatter(
            grad_keys.reshape(head_groups, seq_length, grouped_keys * HEAD_SIZE).astype(
                jnp.bfloat16
            ),
            "blk",
            scatter_dimension=1,
            tiled=True,
        ).astype(jnp.float32),
        lax.psum_scatter(
            grad_values.reshape(head_groups, seq_length, grouped_keys * HEAD_SIZE).astype(
                jnp.bfloat16
            ),
            "blk",
            scatter_dimension=1,
            tiled=True,
        ).astype(jnp.float32),
    )
    query_grad_low = (
        rotary_embedding(
            grad_query.reshape(
                head_groups, query_rows, grouped_keys * query_per_key_head, HEAD_SIZE
            ),
            query_place,
            -1.0,
        )
        .astype(jnp.bfloat16)
        .reshape(head_groups, query_rows, grouped_keys * query_per_key_head * HEAD_SIZE)
    )
    key_grad_low = (
        rotary_embedding(
            key_own.reshape(head_groups, query_rows, grouped_keys, HEAD_SIZE), query_place, -1.0
        )
        .astype(jnp.bfloat16)
        .reshape(head_groups, query_rows, grouped_keys * HEAD_SIZE)
    )
    value_grad_low = value_own.astype(jnp.bfloat16)
    query_back, key_pullback, value_pullback = (
        lax.all_to_all(query_grad_low, "head", split_axis=1, concat_axis=2, tiled=True),
        lax.all_to_all(key_grad_low, "head", split_axis=1, concat_axis=2, tiled=True),
        lax.all_to_all(value_grad_low, "head", split_axis=1, concat_axis=2, tiled=True),
    )
    query_flat = query_back.reshape(number_of_tokens, QUERY_HEADS * HEAD_SIZE)
    flattened_keys = key_pullback.reshape(number_of_tokens, KEY_VALUE_HEADS * HEAD_SIZE)
    flattened_values = value_pullback.reshape(number_of_tokens, KEY_VALUE_HEADS * HEAD_SIZE)
    query_weight_grad = jnp.dot(attn_in.T, query_flat, preferred_element_type=jnp.float32)
    key_weight_grad = jnp.dot(attn_in.T, flattened_keys, preferred_element_type=jnp.float32)
    value_weight_grad = jnp.dot(attn_in.T, flattened_values, preferred_element_type=jnp.float32)
    attn_in_grad = (
        jnp.dot(query_flat, query_full.T, preferred_element_type=jnp.float32)
        + jnp.dot(flattened_keys, key_full.T, preferred_element_type=jnp.float32)
        + jnp.dot(flattened_values, value_full.T, preferred_element_type=jnp.float32)
    )
    input_part, attn_gain_grad = attn_pull(attn_in_grad)
    token_grad = (residual_grad + input_part).reshape(head_groups, number_of_rows, width_dim)
    (
        query_shard,
        key_shard,
        value_shard,
        out_shard,
        router_shard,
        attn_gain_shard,
        moe_gain_shard,
    ) = (
        lax.psum_scatter(
            query_weight_grad.astype(jnp.bfloat16), ("blk", "head"), scatter_dimension=0, tiled=True
        ).astype(jnp.float32),
        lax.psum_scatter(
            key_weight_grad.astype(jnp.bfloat16), ("blk", "head"), scatter_dimension=0, tiled=True
        ).astype(jnp.float32),
        lax.psum_scatter(
            value_weight_grad.astype(jnp.bfloat16), ("blk", "head"), scatter_dimension=0, tiled=True
        ).astype(jnp.float32),
        lax.psum_scatter(
            out_weight_grad.astype(jnp.bfloat16), ("blk", "head"), scatter_dimension=0, tiled=True
        ).astype(jnp.float32),
        lax.psum_scatter(
            router_grad.astype(jnp.bfloat16), ("blk", "head"), scatter_dimension=0, tiled=True
        ).astype(jnp.float32),
        lax.psum_scatter(
            attn_gain_grad.astype(jnp.bfloat16), ("blk", "head"), scatter_dimension=0, tiled=True
        ).astype(jnp.float32),
        lax.psum_scatter(
            moe_gain_grad.astype(jnp.bfloat16), ("blk", "head"), scatter_dimension=0, tiled=True
        ).astype(jnp.float32),
    )
    summed = (
        lax.psum(query_shard.astype(jnp.bfloat16), "group").astype(jnp.float32),
        lax.psum(key_shard.astype(jnp.bfloat16), "group").astype(jnp.float32),
        lax.psum(value_shard.astype(jnp.bfloat16), "group").astype(jnp.float32),
        lax.psum(out_shard.astype(jnp.bfloat16), "group").astype(jnp.float32),
        lax.psum(router_shard.astype(jnp.bfloat16), "group").astype(jnp.float32),
        lax.psum(attn_gain_shard.astype(jnp.bfloat16), "group").astype(jnp.float32),
        lax.psum(moe_gain_shard.astype(jnp.bfloat16), "group").astype(jnp.float32),
        lax.psum(gate_weight_grad.astype(jnp.bfloat16), "group").astype(jnp.float32),
        lax.psum(up_weight_grad.astype(jnp.bfloat16), "group").astype(jnp.float32),
        lax.psum(down_weight_grad.astype(jnp.bfloat16), "group").astype(jnp.float32),
    )
    return (
        mixed,
        token_grad,
        summed[5],
        summed[6],
        summed[0],
        summed[1],
        summed[2],
        summed[3],
        summed[4],
        summed[7],
        summed[8],
        summed[9],
    )


bf16 = jnp.bfloat16
f32 = jnp.float32
MESH_ID = pl.DeviceIdType.MESH
VMEM_LIMIT = 67 * 1000 * 1000
COLOURS = ((0, 96), (96, 80), (176, 80))
LINKS = (("head", 1), ("blk", 1), ("blk", 2), ("group", 2), ("group", 1))
ORDERS = ((0, 1, 2), (1, 2, 0), (2, 0, 1))


def vmem():
    return pl.BlockSpec(memory_space=pltpu.VMEM)


def anywhere():
    return pl.BlockSpec(memory_space=pl.ANY)


def dot_last(left, right):
    return lax.dot_general(left, right, (((1,), (1,)), ((), ())), preferred_element_type=f32)


def dot_first(left, right):
    return lax.dot_general(left, right, (((0,), (0,)), ((), ())), preferred_element_type=f32)


def dot(left, right):
    return jnp.dot(left, right, preferred_element_type=f32)


def my_place():
    return lax.axis_index("blk") * 2 + lax.axis_index("head")


def peer(step):
    place = lax.rem(my_place() + step, 8)
    return place, {"blk": place // 2, "head": lax.rem(place, 2)}


def neighbour(link):
    if link == 0:
        return {"head": 1 - lax.axis_index("head")}
    blk = lax.axis_index("blk")
    if link == 1:
        return {"blk": blk + 1 - 2 * lax.rem(blk, 2)}
    return {"blk": lax.rem(blk + 2, 4)}


def my_bits():
    blk = lax.axis_index("blk")
    return (lax.axis_index("head"), lax.rem(blk, 2), blk // 2)


def meet_all():
    barrier = pltpu.get_barrier_semaphore()
    for step in range(1, 8):
        pl.semaphore_signal(barrier, 1, device_id=peer(step)[1], device_id_type=MESH_ID)
    pl.semaphore_wait(barrier, 7)


def remote(src, dst, send, recv, target):
    return pltpu.make_async_remote_copy(
        src_ref=src, dst_ref=dst, send_sem=send, recv_sem=recv, device_id=target, device_id_type=MESH_ID
    )


def cube_index(bits, fixed, rows):
    entries = [pl.ds(fixed[link], 1) if link in fixed else pl.ds(0, 2) for link in (2, 1, 0)]
    return tuple(entries) + (pl.ds(*rows),)


def lanes(shape):
    return lax.broadcasted_iota(jnp.int32, shape, len(shape) - 1)


def turned(u):
    low = lax.rem(lanes(u.shape), 64) < 32
    return jnp.where(low, -pltpu.roll(u, 96, 1), pltpu.roll(u, 32, 1))


def two_heads(q):
    low = lanes(q.shape) < 64
    return jnp.concatenate([jnp.where(low, q, 0.0), jnp.where(low, pltpu.roll(q, 64, 1), 0.0)], 0)


def two_heads_high(g):
    high = lanes(g.shape) >= 64
    return jnp.concatenate([jnp.where(high, pltpu.roll(g, 64, 1), 0.0), jnp.where(high, g, 0.0)], 0)


def block_probability(q_ref, kv_ref, docs, segs, s, i):
    short = isinstance(i, int)
    first = 0 if short else pl.multiple_of((i - 4) * 128, 128)
    count = (i + 1) * 128 if short else 640
    mine = pl.ds(i * 128 if short else pl.multiple_of(i * 128, 128), 128)
    q2 = two_heads(q_ref[s, mine].astype(f32))
    kv = kv_ref[s, pl.ds(first, count)]
    raw = dot_last((q2 * 0.125).astype(bf16), kv)
    q_place = i * 128 + lax.broadcasted_iota(jnp.int32, (128, count), 0)
    k_place = first + lanes((128, count))
    q_doc = docs[s, mine]
    keys = pl.ds(first, count)
    k_doc = jnp.where(s == 0, segs[0:1, keys], segs[1:2, keys]).astype(f32)
    allowed = (q_place >= k_place) & (q_doc == k_doc)
    allowed = jnp.concatenate([allowed, allowed], 0)
    masked = jnp.where(allowed, raw, masked_out)
    top = jnp.max(masked, -1, keepdims=True)
    weight = jnp.exp(masked - top)
    probability = weight * (1.0 / jnp.sum(weight, -1, keepdims=True))
    return first, count, q2, kv, probability


def norm_back(values, gain, grad):
    scale = lax.rsqrt(jnp.mean(values * values, -1, keepdims=True) + epsilon)
    inner = grad * gain
    along = jnp.mean(values * inner, -1, keepdims=True)
    out = scale * inner - values * (scale * scale * scale * along)
    gain_grad = jnp.sum(grad * values * scale, 0, keepdims=True)
    return out, gain_grad


def expert_inner(rows_e, pair_e, gate_w, up_w, down_w):
    gate_val = dot(rows_e, gate_w)
    up_val = dot(rows_e, up_w)
    sig = 1.0 / (1.0 + jnp.exp(-gate_val))
    silu = gate_val * sig
    hidden = (silu * up_val).astype(bf16)
    hidden_grad = dot_last(pair_e, down_w)
    gate_grad = (hidden_grad * up_val * sig * (1.0 + gate_val * (1.0 - sig))).astype(bf16)
    up_grad = (hidden_grad * silu).astype(bf16)
    return hidden, gate_grad, up_grad


def sibling():
    group = lax.axis_index("group")
    return {"group": group + 1 - 2 * lax.rem(group, 2)}


def mirror():
    return {"group": lax.rem(lax.axis_index("group") + 2, 4)}


def my_core():
    return lax.rem(lax.axis_index("group"), 2)


def meet(targets):
    barrier = pltpu.get_barrier_semaphore()
    for target in targets:
        pl.semaphore_signal(barrier, 1, device_id=target, device_id_type=MESH_ID)
    pl.semaphore_wait(barrier, len(targets))


def peers():
    return [peer(step)[1] for step in range(1, 8)]


def cube_entry(fixed):
    return tuple(pl.ds(fixed[link], 1) if link in fixed else pl.ds(0, 2) for link in (2, 1, 0))


class Gather:
    def __init__(self, items, send, recv):
        self.items, self.send, self.recv, self.bits = items, send, recv, my_bits()

    def copies(self, step):
        made = []
        for k, (src, place, order) in enumerate(self.items):
            fixed = {link: self.bits[link] for link in order[step:]}
            where = place(cube_entry(fixed))
            here = where
            if step == 0:
                here = src
                where = place((self.bits[2], self.bits[1], self.bits[0]))
            made.append(remote(here, where, self.send.at[step, k], self.recv.at[step, k], neighbour(order[step])))
        return made

    def start(self, step):
        for copy in self.copies(step):
            copy.start()

    def wait(self, step):
        for copy in self.copies(step):
            copy.wait_recv()

    def advance(self, step):
        for before, after in zip(self.copies(step - 1), self.copies(step)):
            before.wait_recv()
            after.start()

    def sent(self):
        for step in range(3):
            for copy in self.copies(step):
                copy.wait_send()


SHARES = ((0, 48), (96, 48), (176, 48), (48, 48), (144, 32), (224, 32))
HALF_SHARES = tuple(
    tuple((s * 128 + start, count) for start, count in ((0, 32), (32, 32), (64, 16), (80, 16), (96, 16), (112, 16)))
    for s in range(2)
)


def row_items(src, dst, shares=SHARES):
    def item(k):
        start, count = shares[k]
        return (src.at[pl.ds(start, count)], lambda entry: dst.at[entry + (pl.ds(start, count),)], ORDERS[k % 3])

    return [item(k) for k in range(len(shares))]


ROW_CUTS = tuple((pl.ds(start, count), slice(None)) for start, count in SHARES)


class CubeSum:
    def __init__(self, source, part, cuts, scratch, base=0):
        self.source, self.part, self.cuts = source, part, cuts
        self.kept = tuple((pl.ds(row.start - base, row.size) if base else row, lane) for row, lane in cuts)
        *self.got, self.held0, self.got1, self.held1, self.got2, self.send, self.recv = scratch
        self.bits = my_bits()
        self.orders = [ORDERS[k % 3] for k in range(len(cuts))]

    def copy(self, step, k):
        order, cut, kept = self.orders[k], self.cuts[k], self.kept[k]
        other = 1 - self.bits[order[step]]
        if step == 0:
            src = self.source.at[cube_entry({order[0]: other}) + cut]
            dst = self.got[k]
        elif step == 1:
            src = self.held0.at[(other, slice(None)) + kept]
            dst = self.got1.at[(slice(None),) + kept]
        else:
            src = self.held1.at[(other,) + kept]
            dst = self.got2.at[kept]
        return remote(src, dst, self.send.at[step, k], self.recv.at[step, k], neighbour(order[step]))

    def start(self):
        for k in range(len(self.cuts)):
            self.copy(0, k).start()

    def middle(self):
        for k, order in enumerate(self.orders):
            self.copy(0, k).wait_recv()
            cut, kept = self.cuts[k], self.kept[k]

            def add(w, carry, k=k, order=order, cut=cut, kept=kept):
                u, v = w // 2, lax.rem(w, 2)
                mine = {order[0]: self.bits[order[0]], order[1]: u, order[2]: v}
                there = {order[0]: 0, order[1]: u, order[2]: v}
                landed = self.got[k][there[2], there[1], there[0]].astype(f32)
                here = self.part[(mine[2], mine[1], mine[0]) + cut].astype(f32)
                self.held0[(u, v) + kept] = (here + landed).astype(bf16)
                return carry

            lax.fori_loop(0, 4, add, 0)
            self.copy(1, k).start()

    def last(self):
        for k, order in enumerate(self.orders):
            self.copy(1, k).wait_recv()
            kept = self.kept[k]

            def add(v, carry, order=order, kept=kept):
                here = self.held0[(self.bits[order[1]], v) + kept].astype(f32)
                self.held1[(v,) + kept] = (here + self.got1[(v,) + kept].astype(f32)).astype(bf16)
                return carry

            lax.fori_loop(0, 2, add, 0)
            self.copy(2, k).start()

    def finish(self, store):
        for k, order in enumerate(self.orders):
            self.copy(2, k).wait_recv()
            kept = self.kept[k]
            store(
                self.cuts[k], self.held1[(self.bits[order[2]],) + kept].astype(f32) + self.got2[kept].astype(f32)
            )

    def sent(self):
        for step in range(3):
            for k in range(len(self.cuts)):
                self.copy(step, k).wait_send()


def cube_sum_scratch(rows, width, cuts):
    def share(k):
        row, lane = cuts[k]
        shape = [2, 2, 2, rows if row == slice(None) else row.size, width if lane == slice(None) else lane.size]
        shape[2 - ORDERS[k % 3][0]] = 1
        return pltpu.VMEM(tuple(shape), bf16)

    return [
        *(share(k) for k in range(len(cuts))),
        pltpu.VMEM((2, 2, rows, width), bf16),
        pltpu.VMEM((2, rows, width), bf16),
        pltpu.VMEM((2, rows, width), bf16),
        pltpu.VMEM((rows, width), bf16),
        pltpu.SemaphoreType.DMA((3, len(cuts))),
        pltpu.SemaphoreType.DMA((3, len(cuts))),
    ]


class Spread:
    def __init__(self, src, dst, send, recv):
        self.src, self.dst, self.send, self.recv = src, dst, send, recv

    def copy(self, step):
        place, target = peer(step)
        return remote(self.src(place), self.dst(my_place()), self.send.at[step], self.recv.at[step], target)

    def start(self):
        for step in range(1, 8):
            self.copy(step).start()

    def wait(self):
        for step in range(1, 8):
            self.copy(step).wait()


def rope_tables():
    frequency = 10000.0 ** (-(np.arange(128) % 32) * 2.0 / 64)
    near = np.arange(128)[:, None] * frequency[None, :]
    far = np.arange(8)[:, None] * 128.0 * frequency[None, :]
    return tuple(np.asarray(t, np.float32) for t in (np.cos(near), np.sin(near), np.cos(far), np.sin(far)))


def fill_rope(near_cos, near_sin, far_cos, far_sin, cosine, sine):
    for j in range(8):
        rows = pl.ds(j * 128, 128)
        fc, fs = far_cos[pl.ds(j, 1)], far_sin[pl.ds(j, 1)]
        cosine[rows] = fc * near_cos[...] - fs * near_sin[...]
        sine[rows] = fs * near_cos[...] + fc * near_sin[...]


THIRDS = ((0, 384), (384, 384), (768, 256))


def fill_docs(segs, docs):
    for s in range(2):
        for j in range(8):
            row = segs[pl.ds(s, 1), pl.ds(j * 128, 128)].astype(f32)
            docs[s, pl.ds(j * 128, 128)] = jnp.broadcast_to(row, (128, 128)).T[:, 0:1]


def fill_upper(upper):
    row = lax.broadcasted_iota(jnp.int32, upper.shape, 0)
    upper[...] = jnp.where(row < lanes(upper.shape), 1.0, 0.0).astype(bf16)


def forward_kernel(
    tok, cot, wq, wk, wv, wo, attn_gain, moe_gain, router, routes, segs, near_cos, near_sin, far_cos, far_sin,
    attn_hbm, q_out, kv_out, amix, residual_out, moe_in_out, weights_out, wo_hbm, gains_all, router_all, routes_all,
    cot_hbm, cot_mirror, routes_mirror, wkv,
    tok_all, attn_all, cot_all, wo_all, w_all, mix, cosine, sine, docs, gains,
    tok_send, tok_recv, cot_send, cot_recv, small_send, small_recv, mix_send, mix_recv, wo_send, wo_recv,
    pair_send, pair_recv, own_sem, out_sem,
):
    me, core = my_place(), my_core()
    half = pl.ds(pl.multiple_of(core * 64, 64), 64)
    own_entry = (me // 4, lax.rem(me // 2, 2), lax.rem(me, 2))
    first_row = lax.broadcasted_iota(jnp.int32, (16, 128), 0)
    both_gains = jnp.where(first_row == 1, moe_gain[...].astype(f32), 0.0)
    gains[...] = jnp.where(first_row == 0, attn_gain[...].astype(f32), both_gains).astype(bf16)
    for j in range(4):
        low = lanes((128, 128)) < 64
        k_two, v_two = (w[:, j * 128 : (j + 1) * 128].astype(f32) for w in (wk, wv))
        wkv[:, j * 256 : j * 256 + 128] = jnp.where(low, k_two, pltpu.roll(v_two, 64, 1)).astype(bf16)
        wkv[:, j * 256 + 128 : j * 256 + 256] = jnp.where(low, pltpu.roll(k_two, 64, 1), v_two).astype(bf16)
    meet(peers() + [sibling(), mirror()])
    tok_gather = Gather(row_items(tok, tok_all), tok_send, tok_recv)
    tok_gather.start(0)
    pairs = (
        (lambda j: wq.at[half, pl.ds(j * 128, 128)], lambda i: w_all.at[i, half, pl.ds(0, 128)]),
        (lambda j: wkv.at[half, pl.ds(j * 128, 128)], lambda i: w_all.at[i, half, pl.ds(128, 128)]),
        (lambda j: gains, lambda i: gains_all.at[:, pl.ds(i * 128, 128)]),
        (lambda j: router, lambda i: router_all.at[:, pl.ds(i * 128, 128)]),
        (lambda j: routes.at[:, pl.ds(0, 128)], lambda i: routes_all.at[:, pl.ds(i * 128, 128)]),
        (lambda j: routes.at[:, pl.ds(128, 128)], lambda i: routes_all.at[:, pl.ds(1024 + i * 128, 128)]),
    )
    smalls = [Spread(src, dst, small_send.at[k], small_recv.at[k]) for k, (src, dst) in enumerate(pairs)]
    own = [pltpu.make_async_copy(src(me), dst(me), own_sem.at[k]) for k, (src, dst) in enumerate(pairs)]
    own += [
        pltpu.make_async_copy(tok, tok_all.at[own_entry], own_sem.at[6]),
        pltpu.make_async_copy(cot, cot_all.at[own_entry], own_sem.at[7]),
        pltpu.make_async_copy(wo.at[half], wo_all.at[own_entry + (half,)], own_sem.at[8]),
    ]
    for copy in own:
        copy.start()
    for small in smalls:
        small.start()
    fill_rope(near_cos, near_sin, far_cos, far_sin, cosine, sine)
    for copy in own:
        copy.wait()
    tok_gather.advance(1)
    fill_docs(segs, docs)
    tok_gather.advance(2)
    for small in smalls:
        small.wait()
    w_pair = remote(w_all.at[:, half], w_all.at[:, half], pair_send.at[3], pair_recv.at[3], sibling())
    w_pair.start()
    tok_gather.wait(2)
    w_pair.wait()

    def wo_item(k):
        where = (half, pl.ds(*THIRDS[k]))
        return (wo.at[where], lambda entry: wo_all.at[entry + where], ORDERS[k])

    wo_gather = Gather([wo_item(k) for k in range(3)], wo_send, wo_recv)
    wo_gather.start(0)
    cot_gather = Gather(row_items(cot, cot_all), cot_send, cot_recv)
    cot_gather.start(0)
    cot_copy = remote(cot, cot_mirror, pair_send.at[1], pair_recv.at[1], mirror())
    cot_copy.start()
    routes_copy = remote(routes_all, routes_mirror, pair_send.at[0], pair_recv.at[0], mirror())
    routes_copy.start()

    gain_row = gains_all[0:1].astype(f32)

    def project(j, carry):
        rows = pl.ds(pl.multiple_of(j * 128, 128), 128)
        x = tok_all[j // 4, lax.rem(j // 2, 2), lax.rem(j, 2)].astype(f32)
        scale = lax.rsqrt(jnp.mean(x * x, -1, keepdims=True) + epsilon)
        attn_in = (x * scale * gain_row).astype(bf16)
        attn_all[j] = attn_in
        both = dot(attn_in, w_all[...].reshape(1024, 256))
        c = cosine[rows]
        n = sine[rows]
        c2 = jnp.concatenate([c, c], 0)
        n2 = jnp.concatenate([n, n], 0)
        q = both[:, :128]
        kv = both[:, 128:]
        q = (q * c2 + turned(q) * n2).astype(bf16)
        kv = jnp.where(lanes(kv.shape) < 64, kv * c2 + turned(kv) * n2, kv).astype(bf16)
        for s in range(2):
            q_out[s, rows] = q[s * 128 : (s + 1) * 128]
            kv_out[s, rows] = kv[s * 128 : (s + 1) * 128]
        return carry

    lax.fori_loop(0, 8, project, 0)
    attn_copy = pltpu.make_async_copy(attn_all, attn_hbm, out_sem.at[0])
    attn_copy.start()
    wo_gather.advance(1)
    cot_gather.advance(1)
    wo_pair = remote(
        wo_all.at[:, :, :, half], wo_all.at[:, :, :, half], pair_send.at[2], pair_recv.at[2], sibling()
    )

    def mix_copy(i):
        return remote(
            mix.at[i],
            amix.at[:, :, pl.ds(pl.multiple_of(me * 128, 128), 128)],
            mix_send.at[i],
            mix_recv.at[me],
            {"blk": i // 2, "head": lax.rem(i, 2)},
        )

    def send_mix(i):
        @pl.when(me != i)
        def _():
            mix_copy(i).start()

    def attend_block(i):
        def attend(s, carry):
            first, count, q2, kv, probability = block_probability(q_out, kv_out, docs, segs, s, i)
            mixed = dot(probability.astype(bf16), kv)
            low = lanes((128, 128)) < 64
            mix[i, s] = jnp.where(low, pltpu.roll(mixed[:128], 64, 1), mixed[128:]).astype(bf16)
            return carry

        lax.fori_loop(0, 2, attend, 0)

    for i in range(4):
        attend_block(i)
        if i > 0:
            send_mix(i - 1)
        if i == 2:
            wo_gather.advance(2)

    def attend_long(i, carry):
        attend_block(i)
        send_mix(i - 1)

        @pl.when(i == 4)
        def _():
            cot_gather.advance(2)

        return carry

    lax.fori_loop(4, 8, attend_long, 0)
    send_mix(7)
    wo_gather.wait(2)
    wo_pair.start()
    mine = pltpu.make_async_copy(
        mix.at[me], amix.at[:, :, pl.ds(pl.multiple_of(me * 128, 128), 128)], own_sem.at[0]
    )
    mine.start()
    wo_pair.wait()
    wo_copy = pltpu.make_async_copy(wo_all, wo_hbm, out_sem.at[1])
    wo_copy.start()
    for step in range(1, 8):
        place, target = peer(step)
        remote(
            mix.at[place],
            amix.at[:, :, pl.ds(pl.multiple_of(place * 128, 128), 128)],
            mix_send.at[place],
            mix_recv.at[place],
            target,
        ).wait()
    mine.wait()
    width = tok.shape[-1]
    residual = tok[...].astype(f32) + dot(amix[...].reshape(256, width), wo_all[...].reshape(width, width))
    residual_out[...] = residual
    scale = lax.rsqrt(jnp.mean(residual * residual, -1, keepdims=True) + epsilon)
    moe_in = (residual * scale * gains_all[1:2].astype(f32)).astype(bf16)
    moe_in_out[...] = moe_in
    logits = dot_last(router_all[...], moe_in)
    experts = lax.broadcasted_iota(jnp.int32, logits.shape, 0)
    picked = [
        jnp.sum(jnp.where(experts == routes[pl.ds(k, 1)], logits, 0.0), 0, keepdims=True) for k in range(TOP)
    ]
    picked = jnp.concatenate(picked, 0)
    weight = jnp.exp(picked - jnp.max(picked, 0, keepdims=True))
    weights_out[...] = weight / jnp.sum(weight, 0, keepdims=True)
    cot_gather.wait(2)
    cot_out = pltpu.make_async_copy(cot_all, cot_hbm, out_sem.at[2])
    cot_out.start()
    routes_copy.wait()
    cot_copy.wait()
    tok_gather.sent()
    cot_gather.sent()
    wo_gather.sent()
    attn_copy.wait()
    wo_copy.wait()
    cot_out.wait()


def forward(*values):
    tok = values[0]
    width = tok.shape[-1]
    tables = tuple(jnp.asarray(t) for t in rope_tables())
    return pl.pallas_call(
        forward_kernel,
        out_shape=(
            jax.ShapeDtypeStruct((8, 256, width), bf16),
            jax.ShapeDtypeStruct((2, 1024, 128), bf16),
            jax.ShapeDtypeStruct((2, 1024, 128), bf16),
            jax.ShapeDtypeStruct((2, 128, width), bf16),
            jax.ShapeDtypeStruct((256, width), f32),
            jax.ShapeDtypeStruct((256, width), bf16),
            jax.ShapeDtypeStruct((8, 256), f32),
            jax.ShapeDtypeStruct((2, 2, 2, 128, width), bf16),
            jax.ShapeDtypeStruct((16, width), bf16),
            jax.ShapeDtypeStruct((32, width), bf16),
            jax.ShapeDtypeStruct((8, 2048), jnp.int32),
            jax.ShapeDtypeStruct((2, 2, 2, 256, width), bf16),
            jax.ShapeDtypeStruct((256, width), bf16),
            jax.ShapeDtypeStruct((8, 2048), jnp.int32),
            jax.ShapeDtypeStruct((128, 1024), bf16),
        ),
        in_specs=[vmem()] * 15,
        out_specs=(
            anywhere(), vmem(), vmem(), vmem(), vmem(), vmem(), vmem(), anywhere(), vmem(), vmem(), vmem(),
            anywhere(), vmem(), vmem(), vmem(),
        ),
        scratch_shapes=[
            pltpu.VMEM((2, 2, 2, 256, width), bf16),
            pltpu.VMEM((8, 256, width), bf16),
            pltpu.VMEM((2, 2, 2, 256, width), bf16),
            pltpu.VMEM((2, 2, 2, 128, width), bf16),
            pltpu.VMEM((8, 128, 256), bf16),
            pltpu.VMEM((8, 2, 128, 128), bf16),
            pltpu.VMEM((1024, 128), f32),
            pltpu.VMEM((1024, 128), f32),
            pltpu.VMEM((2, 1024, 1), f32),
            pltpu.VMEM((16, 128), bf16),
            pltpu.SemaphoreType.DMA((3, 6)),
            pltpu.SemaphoreType.DMA((3, 6)),
            pltpu.SemaphoreType.DMA((3, 6)),
            pltpu.SemaphoreType.DMA((3, 6)),
            pltpu.SemaphoreType.DMA((6, 8)),
            pltpu.SemaphoreType.DMA((6, 8)),
            pltpu.SemaphoreType.DMA((8,)),
            pltpu.SemaphoreType.DMA((8,)),
            pltpu.SemaphoreType.DMA((3, 3)),
            pltpu.SemaphoreType.DMA((3, 3)),
            pltpu.SemaphoreType.DMA((4,)),
            pltpu.SemaphoreType.DMA((4,)),
            pltpu.SemaphoreType.DMA((9,)),
            pltpu.SemaphoreType.DMA((3,)),
        ],
        compiler_params=pltpu.CompilerParams(
            collective_id=0, has_side_effects=True, vmem_limit_bytes=VMEM_LIMIT
        ),
        name="forward",
    )(*values, *tables)


SLOT = 4 * CAPH
SPAN = 512
TAKEN = 4 * SLOT


def build_rows(routes, upper, plain, first_expert, block):
    columns = pl.ds(pl.multiple_of(block * SPAN, SPAN), SPAN)
    chosen = routes[:, columns]
    masks = [jnp.max((chosen == first_expert + e).astype(f32), 0, keepdims=True) for e in range(4)]
    mask = jnp.concatenate(masks + [jnp.zeros((4, SPAN), f32)], 0)
    rank = dot(mask.astype(bf16), upper[...])
    slots = lax.broadcasted_iota(jnp.int32, (SLOT, SPAN), 0).astype(f32)
    for e in range(4):
        hit = (slots == rank[e : e + 1]) & (mask[e : e + 1] > 0.0)
        plain[block, e * SLOT : (e + 1) * SLOT] = jnp.where(hit, 1.0, 0.0).astype(bf16)


def slot_weights(routes, weights, plain, column, first_expert, block):
    columns = pl.ds(pl.multiple_of(block * SPAN, SPAN), SPAN)
    chosen = routes[:, columns]
    weight = weights[:, columns]
    for e in range(4):
        share = jnp.sum(jnp.where(chosen == first_expert + e, weight, 0.0), 0, keepdims=True)
        mine = pl.ds(e * SLOT, SLOT)
        column[block, mine] = jnp.sum(plain[block, mine].astype(f32) * share, -1, keepdims=True)


def place_rows(source, block):
    width = source.shape[-1]
    rows = pl.ds(pl.multiple_of((block // 2) * 128, 128), 128)
    return source[lax.rem(block, 2), :, :, rows].reshape(SPAN, width)


def expert_rows(e):
    return pl.ds(pl.multiple_of(e * SLOT, 16), SLOT)


def experts_kernel(
    moe_in, my_weights, cot_mirror, cot_hbm, routes, routes_mirror, gate_hbm, up_hbm, down_hbm,
    out_part, in_sum, p_all, rows_out, pair_out, hidden_out, gate_out, up_out, plain_mirror, pair_mirror, moe_mirror,
    weights_other,
    x, c, cm, upper, plain, rows, pair_grad, pair_in, column, p_col, weights, p_part,
    gate, up, down, hid_buf, gg_buf, ug_buf, part_buf,
    row_send, row_recv, cm_send, cm_recv, w_send, w_recv, p_send, p_recv, pair_send, pair_recv,
    sem_c, sem_w, sem_rows, sem_h, sem_part, own_sem, *sums,
):
    me = my_place()
    first = me * 4
    width = x.shape[-1]
    count = 2 * SLOT
    own_entry = (me // 4, lax.rem(me // 2, 2), lax.rem(me, 2))
    meet(peers() + [mirror()])
    gathers = [
        Gather(row_items(moe_in, x, HALF_SHARES[s]), row_send.at[s], row_recv.at[s]) for s in range(2)
    ]
    gathers[0].start(0)

    def weight_lanes(s, i):
        return weights.at[:, pl.ds(pl.multiple_of(s * 1024 + i * 128, 128), 128)]

    own = [
        pltpu.make_async_copy(moe_in, x.at[own_entry], own_sem.at[0]),
        pltpu.make_async_copy(my_weights.at[:, pl.ds(0, 128)], weight_lanes(0, me), own_sem.at[1]),
        pltpu.make_async_copy(my_weights.at[:, pl.ds(128, 128)], weight_lanes(1, me), own_sem.at[2]),
        pltpu.make_async_copy(cot_mirror, cm.at[own_entry], own_sem.at[3]),
    ]
    for copy in own:
        copy.start()
    weight_spreads = [
        Spread(
            lambda j, s=s: my_weights.at[:, pl.ds(s * 128, 128)],
            lambda i, s=s: weight_lanes(s, i),
            w_send.at[s],
            w_recv.at[s],
        )
        for s in range(2)
    ]
    for spread in weight_spreads:
        spread.start()
    load_c = pltpu.make_async_copy(cot_hbm, c, sem_c)
    load_c.start()

    def fetch(e, slot):
        return [
            pltpu.make_async_copy(gate_hbm.at[e], gate.at[slot], sem_w.at[slot, 0]),
            pltpu.make_async_copy(up_hbm.at[e], up.at[slot], sem_w.at[slot, 1]),
            pltpu.make_async_copy(down_hbm.at[e], down.at[slot], sem_w.at[slot, 2]),
        ]

    for copy in fetch(0, 0):
        copy.start()
    fill_upper(upper)

    def build(block, carry):
        build_rows(routes, upper, plain, first, block)
        return carry

    lax.fori_loop(0, 2, build, 0)
    for copy in own:
        copy.wait()
    gathers[0].advance(1)
    lax.fori_loop(2, 4, build, 0)
    load_c.wait()

    def take_c(block, carry):
        pair_grad[block] = dot(plain[block], place_rows(c, block)).astype(bf16)
        return carry

    gathers[0].advance(2)
    gathers[1].start(0)
    lax.fori_loop(0, 4, take_c, 0)
    for spread in weight_spreads:
        spread.wait()
    weights_copy = remote(weights, weights_other, pair_send.at[0], pair_recv.at[0], mirror())
    weights_copy.start()

    def weigh(block, carry):
        slot_weights(routes, weights, plain, column, first, block)
        return carry

    lax.fori_loop(0, 4, weigh, 0)
    cm_gather = Gather(row_items(cot_mirror, cm), cm_send, cm_recv)
    moe_copy = remote(moe_in, moe_mirror, pair_send.at[1], pair_recv.at[1], mirror())
    p_part[...] = jnp.zeros_like(p_part)

    def take_x(block, carry):
        rows[block] = dot(plain[block], place_rows(x, block)).astype(bf16)
        return carry

    def keep_rows(s):
        pair = pl.ds(2 * s, 2)
        return pltpu.make_async_copy(rows.at[pair], rows_out.at[pair], sem_rows.at[s])

    def keep(s, e, slot):
        where = pl.ds(pl.multiple_of(s * count, 16), count)
        return [
            pltpu.make_async_copy(hid_buf.at[slot], hidden_out.at[e, where], sem_h.at[slot, 0]),
            pltpu.make_async_copy(gg_buf.at[slot], gate_out.at[e, where], sem_h.at[slot, 1]),
            pltpu.make_async_copy(ug_buf.at[slot], up_out.at[e, where], sem_h.at[slot, 2]),
        ]

    def total_of(s):
        cuts = tuple((pl.ds(*cut), slice(None)) for cut in HALF_SHARES[s])
        return CubeSum(x, x, cuts, sums[12 * s : 12 * s + 12], s * 128)

    totals = [total_of(s) for s in range(2)]

    def store(cut, value):
        in_sum[cut] = value

    def one_half(s, carry):
        for t in range(2):

            @pl.when(s == t)
            def _(t=t):
                gathers[t].wait(2)
                if t == 0:
                    gathers[1].advance(1)

        lax.fori_loop(2 * s, 2 * s + 2, take_x, 0)
        keep_rows(s).start()

        @pl.when(s == 0)
        def _():
            gathers[1].advance(2)
            cm_gather.start(0)
            moe_copy.start()

        def expert(e, inner):
            slot = lax.rem(e, 2)
            mine = expert_rows(e)
            pair = pl.ds(2 * s, 2)
            for copy in fetch(e, slot):
                copy.wait()

            @pl.when(4 * s + e < 7)
            def _():
                for copy in fetch(lax.rem(e + 1, 4), 1 - slot):
                    copy.start()

            rows_e = rows[pair, mine].reshape(count, width)
            weight_e = column[pair, mine].reshape(count, 1)
            pair_e = (pair_grad[pair, mine].reshape(count, width).astype(f32) * weight_e).astype(bf16)
            pair_grad[pair, mine] = pair_e.reshape(2, SLOT, width)
            hidden, gate_grad, up_grad = expert_inner(rows_e, pair_e, gate[slot], up[slot], down[slot])

            @pl.when(e >= 2)
            def _():
                for copy in keep(s, e - 2, slot):
                    copy.wait()

            hid_buf[slot] = hidden
            gg_buf[slot] = gate_grad
            ug_buf[slot] = up_grad
            for copy in keep(s, e, slot):
                copy.start()

            @pl.when(e == 0)
            def _():
                keep_rows(s).wait()

            out_e = dot(hidden, down[slot]).astype(bf16).astype(f32)
            p = jnp.sum(out_e * pair_e.astype(f32), -1, keepdims=True)
            p_col[pair, mine] = p.reshape(2, SLOT, 1)
            rows[pair, mine] = (out_e * weight_e).astype(bf16).reshape(2, SLOT, width)
            back = dot_last(gate_grad, gate[slot]) + dot_last(up_grad, up[slot])
            pair_in[pair, mine] = back.astype(bf16).reshape(2, SLOT, width)

            @pl.when(4 * s + e == 3)
            def _():
                cm_gather.advance(1)

            @pl.when(4 * s + e == 5)
            def _():
                cm_gather.advance(2)

            @pl.when(4 * s + e == 6)
            def _():
                totals[0].middle()

            return inner

        lax.fori_loop(0, 4, expert, 0)
        for copy in keep(s, 2, 0) + keep(s, 3, 1):
            copy.wait()
        for t in range(2):

            @pl.when(s == t)
            def _(t=t):
                gathers[t].sent()

        def combine_in(block, inner):
            y = lax.rem(block, 2)
            back = dot_first(plain[block], pair_in[block]).astype(bf16)
            mine = pl.ds(pl.multiple_of(s * 128, 128), 128)
            x[y, :, :, mine] = back.reshape(2, 2, 128, width)
            for e in range(4):
                slots = pl.ds(e * SLOT, SLOT)
                p = jnp.sum(plain[block, slots].astype(f32) * p_col[block, slots], 0, keepdims=True)
                for d in range(4):
                    p_part[y * 4 + d, pl.ds(e, 1), mine] = p[:, d * 128 : (d + 1) * 128]
            return inner

        lax.fori_loop(2 * s, 2 * s + 2, combine_in, 0)
        for t in range(2):

            @pl.when(s == t)
            def _(t=t):
                totals[t].start()
                if t == 1:
                    totals[0].last()

        return carry

    lax.fori_loop(0, 2, one_half, 0)
    keep_pair = pltpu.make_async_copy(pair_grad, pair_out, sem_rows.at[0])
    keep_pair.start()
    p_spread = Spread(lambda j: p_part.at[j], lambda i: p_all.at[i], p_send, p_recv)
    p_spread.start()
    p_own = pltpu.make_async_copy(p_part.at[me], p_all.at[me], own_sem.at[0])
    p_own.start()

    def part_copy(block):
        slot = lax.rem(block, 2)
        rows_of = pl.ds(pl.multiple_of((block // 2) * 128, 128), 128)
        return pltpu.make_async_copy(
            part_buf.at[slot], out_part.at[lax.rem(block, 2), :, :, rows_of], sem_part.at[slot]
        )

    def combine_out(block, carry):
        slot = lax.rem(block, 2)

        @pl.when(block >= 2)
        def _():
            part_copy(block - 2).wait()

        out = dot_first(plain[block], rows[block]).astype(bf16)
        part_buf[slot] = out.reshape(2, 2, 128, width)
        part_copy(block).start()
        return carry

    lax.fori_loop(0, 4, combine_out, 0)
    totals[0].finish(store)
    keep_pair.wait()

    def build_mirror(block, carry):
        build_rows(routes_mirror, upper, plain, first, block)
        return carry

    lax.fori_loop(0, 2, build_mirror, 0)
    totals[1].middle()
    lax.fori_loop(2, 4, build_mirror, 0)
    keep_plain = pltpu.make_async_copy(plain, plain_mirror, sem_rows.at[0])
    keep_plain.start()
    cm_gather.wait(2)

    def take_mirror(block, carry):
        pair_grad[block] = dot(plain[block], place_rows(cm, block)).astype(bf16)
        return carry

    lax.fori_loop(0, 2, take_mirror, 0)
    totals[1].last()
    lax.fori_loop(2, 4, take_mirror, 0)
    keep_mirror = pltpu.make_async_copy(pair_grad, pair_mirror, sem_rows.at[1])
    keep_mirror.start()
    p_spread.wait()
    p_own.wait()
    part_copy(2).wait()
    part_copy(3).wait()
    totals[1].finish(store)
    for total in totals:
        total.sent()
    keep_plain.wait()
    keep_mirror.wait()
    cm_gather.sent()
    weights_copy.wait()
    moe_copy.wait()


def half_cuts(s):
    return tuple((pl.ds(*cut), slice(None)) for cut in HALF_SHARES[s])


def experts(moe_in, my_weights, cot_mirror, cot_all, routes, routes_mirror, gate_w, up_w, down_w):
    width = moe_in.shape[-1]
    ff = gate_w.shape[-1]
    return pl.pallas_call(
        experts_kernel,
        out_shape=(
            jax.ShapeDtypeStruct((2, 2, 2, 256, width), bf16),
            jax.ShapeDtypeStruct((256, width), f32),
            jax.ShapeDtypeStruct((8, 8, 256), f32),
            jax.ShapeDtypeStruct((4, TAKEN, width), bf16),
            jax.ShapeDtypeStruct((4, TAKEN, width), bf16),
            jax.ShapeDtypeStruct((4, TAKEN, ff), bf16),
            jax.ShapeDtypeStruct((4, TAKEN, ff), bf16),
            jax.ShapeDtypeStruct((4, TAKEN, ff), bf16),
            jax.ShapeDtypeStruct((4, TAKEN, SPAN), bf16),
            jax.ShapeDtypeStruct((4, TAKEN, width), bf16),
            jax.ShapeDtypeStruct((256, width), bf16),
            jax.ShapeDtypeStruct((8, 2048), f32),
        ),
        in_specs=[vmem(), vmem(), vmem(), anywhere(), vmem(), vmem(), anywhere(), anywhere(), anywhere()],
        out_specs=(anywhere(), vmem(), vmem()) + (anywhere(),) * 7 + (vmem(), vmem()),
        scratch_shapes=[
            pltpu.VMEM((2, 2, 2, 256, width), bf16),
            pltpu.VMEM((2, 2, 2, 256, width), bf16),
            pltpu.VMEM((2, 2, 2, 256, width), bf16),
            pltpu.VMEM((SPAN, SPAN), bf16),
            pltpu.VMEM((4, TAKEN, SPAN), bf16),
            pltpu.VMEM((4, TAKEN, width), bf16),
            pltpu.VMEM((4, TAKEN, width), bf16),
            pltpu.VMEM((4, TAKEN, width), bf16),
            pltpu.VMEM((4, TAKEN, 1), f32),
            pltpu.VMEM((4, TAKEN, 1), f32),
            pltpu.VMEM((8, 2048), f32),
            pltpu.VMEM((8, 8, 256), f32),
            pltpu.VMEM((2, width, ff), bf16),
            pltpu.VMEM((2, width, ff), bf16),
            pltpu.VMEM((2, ff, width), bf16),
            pltpu.VMEM((2, 2 * SLOT, ff), bf16),
            pltpu.VMEM((2, 2 * SLOT, ff), bf16),
            pltpu.VMEM((2, 2 * SLOT, ff), bf16),
            pltpu.VMEM((2, 2, 2, 128, width), bf16),
            pltpu.SemaphoreType.DMA((2, 3, 6)),
            pltpu.SemaphoreType.DMA((2, 3, 6)),
            pltpu.SemaphoreType.DMA((3, 6)),
            pltpu.SemaphoreType.DMA((3, 6)),
            pltpu.SemaphoreType.DMA((2, 8)),
            pltpu.SemaphoreType.DMA((2, 8)),
            pltpu.SemaphoreType.DMA((8,)),
            pltpu.SemaphoreType.DMA((8,)),
            pltpu.SemaphoreType.DMA((2,)),
            pltpu.SemaphoreType.DMA((2,)),
            pltpu.SemaphoreType.DMA,
            pltpu.SemaphoreType.DMA((2, 3)),
            pltpu.SemaphoreType.DMA((2,)),
            pltpu.SemaphoreType.DMA((2, 3)),
            pltpu.SemaphoreType.DMA((2,)),
            pltpu.SemaphoreType.DMA((4,)),
            *cube_sum_scratch(128, width, half_cuts(0)),
            *cube_sum_scratch(128, width, half_cuts(1)),
        ],
        compiler_params=pltpu.CompilerParams(
            collective_id=1, has_side_effects=True, vmem_limit_bytes=VMEM_LIMIT
        ),
        name="experts",
    )(moe_in, my_weights, cot_mirror, cot_all, routes, routes_mirror, gate_w, up_w, down_w)


LANE_SHARE = 128


def backward_kernel(
    cot, residual, in_sum, p_all, routes, weights, router, moe_in, gains_all, wo_hbm, amix, attn_hbm, q_in, kv_in,
    segs, near_cos, near_sin, far_cos, far_sin, tok, wq, wkv, moe_mirror,
    token_grad, grads, mirror_hbm,
    wo_all, attn_all, wq_all, wkv_all, mm, mix_grad, mg, gq, gkv, gq_rows, gkv_rows, g_all, kv_sum, cosine, sine, docs,
    residual_grad, small_grad,
    w_send, w_recv, mm_send, mm_recv, mg_send, mg_recv, g_send, g_recv, pair_send, pair_recv, own_sem, load_sem,
):
    me, core = my_place(), my_core()
    width = tok.shape[-1]
    meet(peers() + [sibling()])
    half = pl.ds(pl.multiple_of(core * 64, 64), 64)
    own_entry = (me // 4, lax.rem(me // 2, 2), lax.rem(me, 2))
    own = [
        pltpu.make_async_copy(wq.at[half], wq_all.at[own_entry + (half,)], own_sem.at[0]),
        pltpu.make_async_copy(wkv.at[half], wkv_all.at[own_entry + (half,)], own_sem.at[1]),
        pltpu.make_async_copy(moe_mirror, mm.at[own_entry], own_sem.at[2]),
    ]
    loads = [
        pltpu.make_async_copy(wo_hbm, wo_all, load_sem.at[0]),
        pltpu.make_async_copy(attn_hbm, attn_all, load_sem.at[1]),
    ]
    for copy in own + loads:
        copy.start()

    def weight_item(src, dst, start, count, order):
        rows = pl.ds(pl.multiple_of(core * 64 + start, 16), count)
        return (src.at[rows], lambda entry: dst.at[entry + (rows,)], order)

    w_gather = Gather(
        [
            weight_item(wq, wq_all, 0, 48, ORDERS[0]),
            weight_item(wq, wq_all, 48, 16, ORDERS[1]),
            weight_item(wkv, wkv_all, 0, 32, ORDERS[1]),
            weight_item(wkv, wkv_all, 32, 32, ORDERS[2]),
        ],
        w_send,
        w_recv,
    )
    w_gather.start(0)
    mm_gather = Gather(row_items(moe_mirror, mm), mm_send, mm_recv)
    mm_gather.start(0)
    ids = lax.broadcasted_iota(jnp.int32, (32, 256), 0)
    dense = jnp.zeros((32, 256), f32)
    for k in range(TOP):
        dense = dense + jnp.where(ids == routes[pl.ds(k, 1)], weights[pl.ds(k, 1)], 0.0)
    p = jnp.concatenate([p_all[i, 0:4] for i in range(8)], 0)
    logit_grad = (p - dense * jnp.sum(p, 0, keepdims=True)).astype(bf16)
    moe_in_grad = in_sum[...] + dot_first(logit_grad, router[...])
    part, moe_gain_grad = norm_back(residual[...], gains_all[1:2].astype(f32), moe_in_grad)
    total = cot[...].astype(f32) + part
    residual_grad[...] = total
    low_grad = total.astype(bf16)
    for copy in loads[:1]:
        copy.wait()
    back = dot_last(low_grad, wo_all[...].reshape(width, width)).astype(bf16)
    for j in range(8):
        mix_grad[j] = back[:, j * 128 : (j + 1) * 128].reshape(2, 128, 128)
    mix_spread = Spread(lambda j: mix_grad.at[j], lambda i: mg.at[i], mg_send, mg_recv)
    mix_spread.start()
    mix_own = pltpu.make_async_copy(mix_grad.at[me], mg.at[me], own_sem.at[3])
    mix_own.start()
    for copy in own:
        copy.wait()
    w_gather.advance(1)
    fill_rope(near_cos, near_sin, far_cos, far_sin, cosine, sine)
    fill_docs(segs, docs)
    wo_grad = dot_first(amix[...].reshape(256, width), low_grad)
    grads[:, :, 0:width] = wo_grad.astype(bf16).reshape(8, 128, width)
    padded = jnp.concatenate([logit_grad, jnp.zeros((LANE_SHARE - 32, 256), bf16)], 0)
    small_grad[...] = lax.dot_general(moe_in[...], padded, (((0,), (1,)), ((), ())), preferred_element_type=f32)
    mix_spread.wait()
    mix_own.wait()
    mm_gather.advance(1)

    def lane_block(i):
        return pl.ds(pl.multiple_of(i * 128, 128), 128)

    def spread_of(s):
        return [
            Spread(lambda j: gq.at[j, s], lambda i: gq_rows.at[s, :, lane_block(i)], g_send.at[2 * s], g_recv.at[2 * s]),
            Spread(
                lambda j: gkv.at[j, s],
                lambda i: gkv_rows.at[s, :, lane_block(i)],
                g_send.at[2 * s + 1],
                g_recv.at[2 * s + 1],
            ),
        ]

    def own_blocks(s):
        return [
            pltpu.make_async_copy(gq.at[me, s], gq_rows.at[s, :, lane_block(me)], own_sem.at[4 + 2 * s]),
            pltpu.make_async_copy(gkv.at[me, s], gkv_rows.at[s, :, lane_block(me)], own_sem.at[5 + 2 * s]),
        ]

    def attend(s, carry):
        kv_sum[...] = jnp.zeros_like(kv_sum)

        def back_block(i):
            first, count, q2, kv, probability = block_probability(q_in, kv_in, docs, segs, s, i)
            g2 = two_heads_high(mg[i, s].astype(f32)).astype(bf16)
            prob_grad = dot_last(g2, kv)
            delta = jnp.sum(probability * prob_grad, -1, keepdims=True)
            score_grad = (probability * (prob_grad - delta) * 0.125).astype(bf16)
            dq = dot(score_grad, kv)
            keys = pl.ds(first, count)
            kv_sum[keys] += dot_first(score_grad, q2.astype(bf16)) + dot_first(probability.astype(bf16), g2)
            low = lanes((128, 128)) < 64
            dq = jnp.where(low, dq[:128], pltpu.roll(dq[128:], 64, 1))
            rows = pl.ds(i * 128 if isinstance(i, int) else pl.multiple_of(i * 128, 128), 128)
            dq = (dq * cosine[rows] - turned(dq) * sine[rows]).astype(bf16)
            gq[i, s] = dq
            g_all[i, s, :, 0:128] = dq

        for i in range(4):
            back_block(i)
            if i == 2:

                @pl.when(s == 0)
                def _():
                    w_gather.advance(2)

        def back_long(i, inner):
            back_block(i)

            @pl.when(s * 8 + i == 6)
            def _():
                mm_gather.advance(2)

            return inner

        lax.fori_loop(4, 8, back_long, 0)

        def keys_back(i, inner):
            rows = pl.ds(pl.multiple_of(i * 128, 128), 128)
            dkv = kv_sum[rows]
            low = lanes((128, 128)) < 64
            dkv = jnp.where(low, dkv * cosine[rows] - turned(dkv) * sine[rows], dkv).astype(bf16)
            gkv[i, s] = dkv
            g_all[i, s, :, 128:256] = dkv
            return inner

        lax.fori_loop(0, 8, keys_back, 0)
        for spread in spread_of(s):
            spread.start()
        for copy in own_blocks(s):
            copy.start()
        return carry

    lax.fori_loop(0, 2, attend, 0)
    keep_own = own_blocks(0) + own_blocks(1)
    w_gather.wait(2)
    shared = [
        remote(w.at[:, :, :, half], w.at[:, :, :, half], pair_send.at[k], pair_recv.at[k], sibling())
        for k, w in enumerate((wq_all, wkv_all))
    ]
    for copy in shared:
        copy.start()
    loads[1].wait()
    w_grad = dot_first(attn_all[...].reshape(2048, width), g_all[...].reshape(2048, 256))
    grads[:, :, width + LANE_SHARE :] = w_grad.astype(bf16).reshape(8, 128, 256)
    for copy in shared + keep_own:
        copy.wait()
    for s in range(2):
        for spread in spread_of(s):
            spread.wait()
    back = dot_last(gq_rows[...].reshape(256, 1024), wq_all[...].reshape(width, 1024))
    back = back + dot_last(gkv_rows[...].reshape(256, 1024), wkv_all[...].reshape(width, 1024))
    part, attn_gain_grad = norm_back(tok[...].astype(f32), gains_all[0:1].astype(f32), back)
    token_grad[...] = residual_grad[...] + part
    row = lax.broadcasted_iota(jnp.int32, (LANE_SHARE, width), 0)
    gain_rows = jnp.where(row == 32, moe_gain_grad, jnp.where(row == 33, attn_gain_grad, 0.0))
    grads[:, :, width : width + LANE_SHARE] = (small_grad[...] + gain_rows.T).astype(bf16).reshape(8, 128, LANE_SHARE)
    mm_gather.wait(2)
    mm_out = pltpu.make_async_copy(mm, mirror_hbm, load_sem.at[0])
    mm_out.start()
    w_gather.sent()
    mm_gather.sent()
    mm_out.wait()


def backward(*values):
    tok = values[15]
    width = tok.shape[-1]
    tables = tuple(jnp.asarray(t) for t in rope_tables())
    values = values[:15] + tables + values[15:]
    specs = [vmem()] * 23
    specs[9] = specs[11] = anywhere()
    return pl.pallas_call(
        backward_kernel,
        out_shape=(
            jax.ShapeDtypeStruct((256, width), f32),
            jax.ShapeDtypeStruct((8, 128, width + 256 + LANE_SHARE), bf16),
            jax.ShapeDtypeStruct((2, 2, 2, 256, width), bf16),
        ),
        in_specs=specs,
        out_specs=(vmem(), vmem(), anywhere()),
        scratch_shapes=[
            pltpu.VMEM((2, 2, 2, 128, width), bf16),
            pltpu.VMEM((8, 256, width), bf16),
            pltpu.VMEM((2, 2, 2, 128, width), bf16),
            pltpu.VMEM((2, 2, 2, 128, width), bf16),
            pltpu.VMEM((2, 2, 2, 256, width), bf16),
            pltpu.VMEM((8, 2, 128, 128), bf16),
            pltpu.VMEM((8, 2, 128, 128), bf16),
            pltpu.VMEM((8, 2, 128, 128), bf16),
            pltpu.VMEM((8, 2, 128, 128), bf16),
            pltpu.VMEM((2, 128, 1024), bf16),
            pltpu.VMEM((2, 128, 1024), bf16),
            pltpu.VMEM((8, 2, 128, 256), bf16),
            pltpu.VMEM((1024, 128), f32),
            pltpu.VMEM((1024, 128), f32),
            pltpu.VMEM((1024, 128), f32),
            pltpu.VMEM((2, 1024, 1), f32),
            pltpu.VMEM((256, width), f32),
            pltpu.VMEM((width, LANE_SHARE), f32),
            pltpu.SemaphoreType.DMA((3, 4)),
            pltpu.SemaphoreType.DMA((3, 4)),
            pltpu.SemaphoreType.DMA((3, 6)),
            pltpu.SemaphoreType.DMA((3, 6)),
            pltpu.SemaphoreType.DMA((8,)),
            pltpu.SemaphoreType.DMA((8,)),
            pltpu.SemaphoreType.DMA((4, 8)),
            pltpu.SemaphoreType.DMA((4, 8)),
            pltpu.SemaphoreType.DMA((2,)),
            pltpu.SemaphoreType.DMA((2,)),
            pltpu.SemaphoreType.DMA((8,)),
            pltpu.SemaphoreType.DMA((2,)),
        ],
        compiler_params=pltpu.CompilerParams(
            collective_id=2, has_side_effects=True, vmem_limit_bytes=VMEM_LIMIT
        ),
        name="backward",
    )(*values)


SUM_CUTS = tuple((slice(None), pl.ds(k * 384, 384)) for k in range(3))


def expert_weights_kernel(
    x_hbm, plain_hbm, pair_raw, routes, weights, gate_hbm, up_hbm, down_hbm, rows_hbm, pair_hbm, hidden_hbm, gg_hbm, ug_hbm,
    out_part, residual, grads,
    gate_own, up_own, down_own, gate_other, up_other, down_other, mixed, shares,
    x, c, plain, rows, pair_grad, column, gate, up, down,
    both_rows, both_pair, both_hidden, both_gate, gate_buf, up_buf, down_buf,
    g0, g1, g2, g3, g4, g5, got1, got2, sum_send, sum_recv,
    s0, s1, s2, sheld0, sgot1, sheld1, sgot2, ssend, srecv,
    core_got, core_sum, core_qkv, all_got, side_sum, side_got,
    grad_send, grad_recv, core_send, core_recv, part_send, part_recv,
    sem_x, sem_w, sem_own, sem_out, own_sem,
):
    me, core = my_place(), my_core()
    first = me * 4
    side = lax.axis_index("group") // 2
    other = 1 - side
    width = x.shape[-1]
    ff = gate.shape[-1]
    half = pl.ds(pl.multiple_of(core * 64, 64), 64)
    other_half = pl.ds(pl.multiple_of((1 - core) * 64, 64), 64)
    meet(peers() + [sibling(), mirror()])
    core_copy = remote(grads.at[:, other_half], core_got, core_send.at[0], core_recv.at[0], sibling())
    core_copy.start()
    total = CubeSum(
        out_part, x, ROW_CUTS, (g0, g1, g2, g3, g4, g5, c.at[pl.ds(0, 2)], got1, c.at[2], got2, sum_send, sum_recv)
    )
    total.start()
    loads = [
        pltpu.make_async_copy(plain_hbm, plain, sem_x.at[1]),
        pltpu.make_async_copy(pair_raw, pair_grad, sem_x.at[2]),
        pltpu.make_async_copy(x_hbm, x, sem_x.at[0]),
    ]
    for copy in loads:
        copy.start()

    def fetch(e, slot):
        return [
            pltpu.make_async_copy(gate_hbm.at[e], gate.at[slot], sem_w.at[slot, 0]),
            pltpu.make_async_copy(up_hbm.at[e], up.at[slot], sem_w.at[slot, 1]),
            pltpu.make_async_copy(down_hbm.at[e], down.at[slot], sem_w.at[slot, 2]),
        ]

    for copy in fetch(0, 0):
        copy.start()
    loads[0].wait()

    def weigh(block, carry):
        slot_weights(routes, weights, plain, column, first, block)
        return carry

    lax.fori_loop(0, 4, weigh, 0)
    core_copy.wait()
    summed = width + LANE_SHARE
    for j in range(8):
        both = (grads[j, half].astype(f32) + core_got[j].astype(f32)).astype(bf16)
        core_sum[j // 4, j // 2 % 2, j % 2] = both[:, :summed]
        core_qkv[j] = both[:, summed:]
    spread = Spread(lambda j: core_qkv.at[j], lambda i: all_got.at[i], grad_send, grad_recv)
    spread.start()
    spread_own = pltpu.make_async_copy(core_qkv.at[me], all_got.at[me], own_sem)
    spread_own.start()
    small_total = CubeSum(
        core_sum, core_sum, SUM_CUTS, (s0, s1, s2, sheld0, sgot1, sheld1, sgot2, ssend, srecv)
    )
    small_total.start()
    for copy in loads[1:]:
        copy.wait()

    def take(block, carry):
        rows[block] = dot(plain[block], place_rows(x, block)).astype(bf16)
        pair_grad[block] = (pair_grad[block].astype(f32) * column[block]).astype(bf16)
        return carry

    lax.fori_loop(0, 4, take, 0)
    load_part = pltpu.make_async_copy(out_part, x, sem_x.at[0])
    load_part.start()
    side_copy = remote(side_sum, side_got, core_send.at[1], core_recv.at[1], mirror())
    last_copy = remote(shares.at[half], shares.at[half], core_send.at[2], core_recv.at[2], sibling())

    def part_copies(e):
        return [
            pltpu.make_async_copy(gate_buf, gate_own.at[e], sem_out.at[0]),
            pltpu.make_async_copy(up_buf, up_own.at[e], sem_out.at[1]),
            pltpu.make_async_copy(down_buf, down_own.at[e], sem_out.at[2]),
            remote(gate_buf, gate_other.at[e], part_send.at[0], part_recv.at[e, 0], sibling()),
            remote(up_buf, up_other.at[e], part_send.at[1], part_recv.at[e, 1], sibling()),
            remote(down_buf, down_other.at[e], part_send.at[2], part_recv.at[e, 2], sibling()),
        ]

    def sent(e):
        made = part_copies(e)
        for copy in made[:3]:
            copy.wait()
        for copy in made[3:]:
            copy.wait_send()

    def expert(e, carry):
        slot = lax.rem(e, 2)
        mine = expert_rows(e)
        own = [
            pltpu.make_async_copy(rows_hbm.at[:, mine], both_rows.at[side], sem_own.at[0]),
            pltpu.make_async_copy(pair_hbm.at[:, mine], both_pair.at[side], sem_own.at[1]),
            pltpu.make_async_copy(hidden_hbm.at[e], both_hidden.at[side], sem_own.at[2]),
            pltpu.make_async_copy(gg_hbm.at[e], both_gate.at[side, :, pl.ds(0, ff)], sem_own.at[3]),
            pltpu.make_async_copy(ug_hbm.at[e], both_gate.at[side, :, pl.ds(ff, ff)], sem_own.at[4]),
        ]
        for copy in own:
            copy.start()
        for copy in fetch(e, slot):
            copy.wait()

        @pl.when(e < 3)
        def _():
            for copy in fetch(e + 1, 1 - slot):
                copy.start()

        rows_e = rows[:, mine].reshape(TAKEN, width)
        pair_e = pair_grad[:, mine].reshape(TAKEN, width)
        hidden, gate_grad, up_grad = expert_inner(rows_e, pair_e, gate[slot], up[slot], down[slot])
        both_rows[other] = rows_e.reshape(4, SLOT, width)
        both_pair[other] = pair_e.reshape(4, SLOT, width)
        both_hidden[other] = hidden
        both_gate[other, :, 0:ff] = gate_grad
        both_gate[other, :, ff : 2 * ff] = up_grad

        for copy in own:
            copy.wait()

        @pl.when(e >= 1)
        def _():
            sent(e - 1)

        sums = dot_first(both_rows[...].reshape(2 * TAKEN, width), both_gate[...].reshape(2 * TAKEN, 2 * ff))
        gate_buf[...] = sums[:, :ff].astype(bf16)
        up_buf[...] = sums[:, ff:].astype(bf16)
        down_buf[...] = dot_first(
            both_hidden[...].reshape(2 * TAKEN, ff), both_pair[...].reshape(2 * TAKEN, width)
        ).astype(bf16)
        for copy in part_copies(e):
            copy.start()

        @pl.when(e == 0)
        def _():
            small_total.middle()
            load_part.wait()
            total.middle()

        @pl.when(e == 1)
        def _():
            small_total.last()
            total.last()

            def keep_sum(cut, value):
                side_sum[cut] = value.astype(bf16)

            small_total.finish(keep_sum)
            spread.wait()
            spread_own.wait()
            for i in range(8):
                side_sum[:, summed + i * 256 : summed + (i + 1) * 256] = all_got[i]
            side_copy.start()

        @pl.when(e == 2)
        def _():
            def store(cut, value):
                mixed[cut] = (residual[cut] + value).astype(bf16)

            total.finish(store)

        return carry

    lax.fori_loop(0, 4, expert, 0)
    side_copy.wait()
    shares[half] = (side_sum[...].astype(f32) + side_got[...].astype(f32)).astype(bf16)
    last_copy.start()
    total.sent()
    small_total.sent()
    last_copy.wait()
    sent(3)
    for e in range(4):
        for copy in part_copies(e)[3:]:
            copy.wait_recv()


def expert_weights(x, plain, pair, routes, weights, gate_w, up_w, down_w, kept, out_part, residual, grads):
    width = gate_w.shape[1]
    ff = gate_w.shape[-1]
    wide = grads.shape[-1]
    out = [jax.ShapeDtypeStruct(w.shape, bf16) for w in (gate_w, up_w, down_w)]
    sums = cube_sum_scratch(256, width, ROW_CUTS)
    return pl.pallas_call(
        expert_weights_kernel,
        out_shape=(
            *out,
            *out,
            jax.ShapeDtypeStruct((256, width), bf16),
            jax.ShapeDtypeStruct((128, width + LANE_SHARE + 2048), bf16),
        ),
        in_specs=[anywhere()] * 3 + [vmem()] * 2 + [anywhere()] * 9 + [vmem()] * 2,
        out_specs=(anywhere(),) * 6 + (vmem(),) * 2,
        scratch_shapes=[
            pltpu.VMEM((2, 2, 2, 256, width), bf16),
            pltpu.VMEM((3, 2, 256, width), bf16),
            pltpu.VMEM((4, TAKEN, SPAN), bf16),
            pltpu.VMEM((4, TAKEN, width), bf16),
            pltpu.VMEM((4, TAKEN, width), bf16),
            pltpu.VMEM((4, TAKEN, 1), f32),
            pltpu.VMEM((2, width, ff), bf16),
            pltpu.VMEM((2, width, ff), bf16),
            pltpu.VMEM((2, ff, width), bf16),
            pltpu.VMEM((2, 4, SLOT, width), bf16),
            pltpu.VMEM((2, 4, SLOT, width), bf16),
            pltpu.VMEM((2, TAKEN, ff), bf16),
            pltpu.VMEM((2, TAKEN, 2 * ff), bf16),
            pltpu.VMEM((width, ff), bf16),
            pltpu.VMEM((width, ff), bf16),
            pltpu.VMEM((ff, width), bf16),
            *sums[:6],
            sums[7],
            sums[9],
            *sums[10:],
            *cube_sum_scratch(64, width + LANE_SHARE, SUM_CUTS),
            pltpu.VMEM((8, 64, wide), bf16),
            pltpu.VMEM((2, 2, 2, 64, width + LANE_SHARE), bf16),
            pltpu.VMEM((8, 64, 256), bf16),
            pltpu.VMEM((8, 64, 256), bf16),
            pltpu.VMEM((64, width + LANE_SHARE + 2048), bf16),
            pltpu.VMEM((64, width + LANE_SHARE + 2048), bf16),
            pltpu.SemaphoreType.DMA((8,)),
            pltpu.SemaphoreType.DMA((8,)),
            pltpu.SemaphoreType.DMA((3,)),
            pltpu.SemaphoreType.DMA((3,)),
            pltpu.SemaphoreType.DMA((3,)),
            pltpu.SemaphoreType.DMA((4, 3)),
            pltpu.SemaphoreType.DMA((3,)),
            pltpu.SemaphoreType.DMA((2, 3)),
            pltpu.SemaphoreType.DMA((5,)),
            pltpu.SemaphoreType.DMA((3,)),
            pltpu.SemaphoreType.DMA,
        ],
        compiler_params=pltpu.CompilerParams(
            collective_id=3, has_side_effects=True, vmem_limit_bytes=VMEM_LIMIT
        ),
        name="expert_weights",
    )(x, plain, pair, routes, weights, gate_w, up_w, down_w, *kept, out_part, residual, grads)


def finish_kernel(
    gate_own, up_own, down_own, gate_other, up_other, down_other, shares, mixed, token_grad,
    gate_out, up_out, down_out, query_out, key_out, value_out, wo_out, router_out, moe_gain_out, attn_gain_out,
    mixed_out, token_out,
):
    for own, other, out in ((gate_own, gate_other, gate_out), (up_own, up_other, up_out), (down_own, down_other, down_out)):
        out[...] = own[...].astype(f32) + other[...].astype(f32)
    mixed_out[...] = mixed[...]
    token_out[...] = token_grad[...]

    @pl.when(pl.program_id(0) == 0)
    def _():
        width = wo_out.shape[-1]
        wo_out[...] = shares[:, 0:width].astype(f32)
        small = shares[:, width : width + LANE_SHARE].astype(f32).T
        router_out[...] = small[0:32]
        moe_gain_out[...] = small[32:33]
        attn_gain_out[...] = small[33:34]
        low = lanes((128, 128)) < 64
        base = width + LANE_SHARE
        for j in range(8):
            query_out[:, j * 128 : (j + 1) * 128] = shares[:, base + j * 256 : base + j * 256 + 128].astype(f32)
        for j in range(4):
            left = shares[:, base + j * 512 + 128 : base + j * 512 + 256].astype(f32)
            right = shares[:, base + j * 512 + 384 : base + j * 512 + 512].astype(f32)
            where = slice(j * 128, (j + 1) * 128)
            key_out[:, where] = jnp.where(low, left, pltpu.roll(right, 64, 1))
            value_out[:, where] = jnp.where(low, pltpu.roll(left, 64, 1), right)


def finish(parts, shares, mixed, token_grad):
    width = parts[0].shape[1]
    steps = parts[0].shape[0]

    def block(shape):
        return pl.BlockSpec((1,) + shape[1:], lambda e: (e, 0, 0))

    def rows(shape):
        return pl.BlockSpec((shape[0] // steps,) + shape[1:], lambda e: (e, 0))

    def whole(shape):
        return pl.BlockSpec(shape, lambda e: (0,) * len(shape))

    small = [(128, 1024), (128, 512), (128, 512), (128, width), (32, LANE_SHARE), (1, LANE_SHARE), (1, LANE_SHARE)]
    return pl.pallas_call(
        finish_kernel,
        grid=(steps,),
        out_shape=tuple(jax.ShapeDtypeStruct(p.shape, f32) for p in parts[:3])
        + tuple(jax.ShapeDtypeStruct(shape, f32) for shape in small)
        + (jax.ShapeDtypeStruct(mixed.shape, bf16), jax.ShapeDtypeStruct(token_grad.shape, f32)),
        in_specs=[block(p.shape) for p in parts] + [whole(shares.shape), rows(mixed.shape), rows(token_grad.shape)],
        out_specs=tuple(block(p.shape) for p in parts[:3])
        + tuple(whole(shape) for shape in small)
        + (rows(mixed.shape), rows(token_grad.shape)),
        compiler_params=pltpu.CompilerParams(vmem_limit_bytes=VMEM_LIMIT),
        name="finish",
    )(*parts, shares, mixed, token_grad)


def fast_on_device(
    tokens, segments, routes, cotangent, attn_gain, moe_gain, query_weight, key_projection_matrix,
    value_projection_matrix, out_weight, router_weight, gate_weight, up_weight, down_weight,
):
    width = tokens.shape[-1]
    tok = tokens.reshape(256, width)
    cot = cotangent.reshape(256, width)
    my_routes = routes.reshape(256, TOP).T
    (
        attn_in, q, kv, amix, residual, moe_in, weights, wo_all, gains_all, router_all, routes_all,
        cot_all, cot_mirror, routes_mirror, wkv,
    ) = forward(
        tok, cot, query_weight, key_projection_matrix, value_projection_matrix, out_weight,
        attn_gain.reshape(1, 128), moe_gain.reshape(1, 128), router_weight.T, my_routes, segments,
    )
    out_part, in_sum, p_all, *kept, plain_mirror, pair_mirror, moe_mirror, weights_mirror = experts(
        moe_in, weights, cot_mirror, cot_all, routes_all, routes_mirror, gate_weight, up_weight, down_weight
    )
    token_grad, grads, moe_mirror_all = backward(
        cot, residual, in_sum, p_all, my_routes, weights, router_all, moe_in, gains_all, wo_all, amix, attn_in,
        q, kv, segments, tok, query_weight, wkv, moe_mirror,
    )
    *parts, mixed, shares = expert_weights(
        moe_mirror_all, plain_mirror, pair_mirror, routes_mirror, weights_mirror, gate_weight, up_weight, down_weight,
        kept, out_part, residual, grads,
    )
    (
        gate_grad, up_grad, down_grad, query_grad, key_grad, value_grad, wo_grad, router_grad, moe_gain_grad,
        attn_gain_grad, mixed, token_grad,
    ) = finish(parts, shares, mixed, token_grad)
    return (
        mixed.reshape(tokens.shape), token_grad.reshape(tokens.shape), attn_gain_grad.reshape(128),
        moe_gain_grad.reshape(128), query_grad, key_grad, value_grad, wo_grad, router_grad.T,
        gate_grad, up_grad, down_grad,
    )


def fits(mesh):
    return dict(mesh.shape) == {"group": 4, "blk": 4, "head": 2}


def solution(mesh):
    placed = (
        P("group", ("blk", "head"), None),
        P("group", None),
        P("group", ("blk", "head"), None),
        P("group", ("blk", "head"), None),
        P(("blk", "head")),
        P(("blk", "head")),
        P(("blk", "head"), None),
        P(("blk", "head"), None),
        P(("blk", "head"), None),
        P(("blk", "head"), None),
        P(("blk", "head"), None),
        P(("blk", "head"), None, None),
        P(("blk", "head"), None, None),
        P(("blk", "head"), None, None),
    )
    return jax.shard_map(
        fast_on_device if fits(mesh) else on_device,
        mesh=mesh,
        in_specs=placed,
        out_specs=(
            P("group", ("blk", "head"), None),
            P("group", ("blk", "head"), None),
            P(("blk", "head")),
            P(("blk", "head")),
            P(("blk", "head"), None),
            P(("blk", "head"), None),
            P(("blk", "head"), None),
            P(("blk", "head"), None),
            P(("blk", "head"), None),
            P(("blk", "head"), None, None),
            P(("blk", "head"), None, None),
            P(("blk", "head"), None, None),
        ),
        check_vma=False,
    )
```

profile of v0, /device:TPU:0, one launch (start us, length us, event | category | flops | bytes accessed | tf_op | source)
XLA Modules:
  0.0 365.4 jit_solution(16606559196609262715)
XLA Ops:
  0.6 96.2 %forward.1 = (bf16[8,256,1024]{2,1,0:T(8,128)(2,1)}, bf16[2,1024,128]{2,1,0:T(8,128)(2,1)}, bf16[2,1024,128]{2,1,0:T(8,128)(2,1)}, bf16[2,128,1024]{2,1,0:T(8,12...) custom-call(bf16[256,1024]{1,0:T(8,128)(2,1)} %bitcast.15, ...), custom_call_target="tpu_custom_call" | custom-call | tf_op jit(solution)/shard_map/forward/pallas_call | solution.py:981
  96.9 110.5 %experts.1 = (bf16[2,2,2,256,1024]{4,3,2,1,0:T(8,128)(2,1)}, f32[256,1024]{1,0:T(8,128)}, f32[8,8,256]{2,1,0:T(8,128)}, bf16[4,576,1024]{2,1,0:T(8,128)(2,1)}, b...) custom-call(bf16[256,1024]{1,0:T(8,128)(2,1)} %get-tuple-element.63., ...), custom_call_target="tpu_custom_call" | custom-call | tf_op jit(solution)/shard_map/experts/pallas_call | solution.py:1364
  207.4 72.1 %backward.1 = (f32[256,1024]{1,0:T(8,128)}, bf16[8,128,1408]{2,1,0:T(8,128)(2,1)}, bf16[2,2,2,256,1024]{4,3,2,1,0:T(8,128)(2,1)}) custom-call(bf16[256,1024]{1,0:T(8,128)(2,1)} %bitcast.14, f32[256,1024]{1,0:T(8,128)} %get-tuple-element.62.residual, f32[256,1024]{1,0:T(8,128)} %get-tuple-element.69.in_sum, f32[8,8,256]{2,1,0:T(8,128)} %get-tuple-element.70.p_all, ...), custom_call_target="tpu_custom_call" | custom-call | tf_op jit(solution)/shard_map/backward/pallas_call | solution.py:1619
  279.6 66.1 %expert_weights.1 = (bf16[4,1024,512]{2,1,0:T(8,128)(2,1)}, bf16[4,1024,512]{2,1,0:T(8,128)(2,1)}, bf16[4,512,1024]{2,1,0:T(8,128)(2,1)}, bf16[4,1024,512]{2,1,0...) custom-call(bf16[2,2,2,256,1024]{4,3,2,1,0:T(8,128)(2,1)} %get-tuple, ...), custom_call_target="tpu_custom_call" | custom-call | tf_op jit(solution)/shard_map/expert_weights/pallas_call | solution.py:1860
  345.7 19.5 %finish.1 = (f32[4,1024,512]{2,1,0:T(8,128)}, f32[4,1024,512]{2,1,0:T(8,128)}, f32[4,512,1024]{2,1,0:T(8,128)}, f32[128,1024]{1,0:T(8,128)}, f32[128,512]{1,0:T(...) custom-call(bf16[4,1024,512]{2,1,0:T(8,128)(2,1)} %get-tuple-element, ...), custom_call_target="tpu_custom_call" | custom-call | tf_op jit(solution)/shard_map/finish/pallas_call | solution.py:1961
where the time goes:
time: 366 us; the launch traced here: 365 us
  Pallas kernels  365 us (100%)
    pallas_call x1, Pallas kernels, experts(): pl.pallas_call(experts_kernel, out_shape=(jax.ShapeDtypeStruct((2, 2, 2,...  111 us
    pallas_call x1, Pallas kernels, forward(): pl.pallas_call(forward_kernel, out_shape=(jax.ShapeDtypeStruct((8, 256, w...  96.2 us
    pallas_call x1, Pallas kernels, backward(): pl.pallas_call(backward_kernel, out_shape=(jax.ShapeDtypeStruct((256, wid...  72.1 us
    pallas_call x1, Pallas kernels, expert_weights(): pl.pallas_call(expert_weights_kernel, out_shape=(*out, *out, jax.ShapeDty...  66.1 us
    pallas_call x1, Pallas kernels, finish(): pl.pallas_call(finish_kernel, grid=(steps,), out_shape=tuple((jax.ShapeDt...  19.5 us

commit v1 on v0

--- a/solution.py
+++ b/solution.py
@@ -832,6 +832,8 @@
     for copy in own:
         copy.wait()
     tok_gather.advance(1)
+    cot_copy = remote(cot, cot_mirror, pair_send.at[1], pair_recv.at[1], mirror())
+    cot_copy.start()
     fill_docs(segs, docs)
     tok_gather.advance(2)
     for small in smalls:
@@ -849,8 +851,6 @@
     wo_gather.start(0)
     cot_gather = Gather(row_items(cot, cot_all), cot_send, cot_recv)
     cot_gather.start(0)
-    cot_copy = remote(cot, cot_mirror, pair_send.at[1], pair_recv.at[1], mirror())
-    cot_copy.start()
     routes_copy = remote(routes_all, routes_mirror, pair_send.at[0], pair_recv.at[0], mirror())
     routes_copy.start()
 

time: 366 us -> 363 us (level)
  Pallas kernels: 365 us -> 361 us
where the time goes in v1:
time: 363 us; the launch traced here: 362 us
  Pallas kernels  361 us (99%)
    pallas_call x1, Pallas kernels, experts(): pl.pallas_call(experts_kernel, out_shape=(jax.ShapeDtypeStruct((2, 2, 2,...  107 us
    pallas_call x1, Pallas kernels, forward(): pl.pallas_call(forward_kernel, out_shape=(jax.ShapeDtypeStruct((8, 256, w...  97.1 us
    pallas_call x1, Pallas kernels, backward(): pl.pallas_call(backward_kernel, out_shape=(jax.ShapeDtypeStruct((256, wid...  71.6 us
    pallas_call x1, Pallas kernels, expert_weights(): pl.pallas_call(expert_weights_kernel, out_shape=(*out, *out, jax.ShapeDty...  65.6 us
    pallas_call x1, Pallas kernels, finish(): pl.pallas_call(finish_kernel, grid=(steps,), out_shape=tuple((jax.ShapeDt...  19.5 us

profile of v1, /device:TPU:0, one launch (start us, length us, event | category | flops | bytes accessed | tf_op | source)
XLA Modules:
  0.0 361.5 jit_solution(1480266972757207912)
XLA Ops:
  0.6 97.1 %forward.1 = (bf16[8,256,1024]{2,1,0:T(8,128)(2,1)}, bf16[2,1024,128]{2,1,0:T(8,128)(2,1)}, bf16[2,1024,128]{2,1,0:T(8,128)(2,1)}, bf16[2,128,1024]{2,1,0:T(8,12...) custom-call(bf16[256,1024]{1,0:T(8,128)(2,1)} %bitcast.15, ...), custom_call_target="tpu_custom_call" | custom-call | tf_op jit(solution)/shard_map/forward/pallas_call | solution.py:981
  97.8 106.9 %experts.1 = (bf16[2,2,2,256,1024]{4,3,2,1,0:T(8,128)(2,1)}, f32[256,1024]{1,0:T(8,128)}, f32[8,8,256]{2,1,0:T(8,128)}, bf16[4,576,1024]{2,1,0:T(8,128)(2,1)}, b...) custom-call(bf16[256,1024]{1,0:T(8,128)(2,1)} %get-tuple-element.63., ...), custom_call_target="tpu_custom_call" | custom-call | tf_op jit(solution)/shard_map/experts/pallas_call | solution.py:1364
  204.6 71.6 %backward.1 = (f32[256,1024]{1,0:T(8,128)}, bf16[8,128,1408]{2,1,0:T(8,128)(2,1)}, bf16[2,2,2,256,1024]{4,3,2,1,0:T(8,128)(2,1)}) custom-call(bf16[256,1024]{1,0:T(8,128)(2,1)} %bitcast.14, f32[256,1024]{1,0:T(8,128)} %get-tuple-element.62.residual, f32[256,1024]{1,0:T(8,128)} %get-tuple-element.69.in_sum, f32[8,8,256]{2,1,0:T(8,128)} %get-tuple-element.70.p_all, ...), custom_call_target="tpu_custom_call" | custom-call | tf_op jit(solution)/shard_map/backward/pallas_call | solution.py:1619
  276.2 65.6 %expert_weights.1 = (bf16[4,1024,512]{2,1,0:T(8,128)(2,1)}, bf16[4,1024,512]{2,1,0:T(8,128)(2,1)}, bf16[4,512,1024]{2,1,0:T(8,128)(2,1)}, bf16[4,1024,512]{2,1,0...) custom-call(bf16[2,2,2,256,1024]{4,3,2,1,0:T(8,128)(2,1)} %get-tuple, ...), custom_call_target="tpu_custom_call" | custom-call | tf_op jit(solution)/shard_map/expert_weights/pallas_call | solution.py:1860
  341.8 19.5 %finish.1 = (f32[4,1024,512]{2,1,0:T(8,128)}, f32[4,1024,512]{2,1,0:T(8,128)}, f32[4,512,1024]{2,1,0:T(8,128)}, f32[128,1024]{1,0:T(8,128)}, f32[128,512]{1,0:T(...) custom-call(bf16[4,1024,512]{2,1,0:T(8,128)(2,1)} %get-tuple-element, ...), custom_call_target="tpu_custom_call" | custom-call | tf_op jit(solution)/shard_map/finish/pallas_call | solution.py:1961
